TPU v7x, 32 devices: a whole 2x2x4 slice. The times are simulated.
32 devices in a mesh: ctx: 16 (over z, y, core), ch: 2 (over x).
Axes of the slice: x: 2, y: 2, z: 4, core: 2. Of those that a mesh axis runs over, the one named last changes fastest.
Arguments:
- projections: bfloat16 [3, 2048, 8192], P(None, 'ctx', 'ch'), may hold values from -150 to 150
- grouped_short_filters: float32 [3, 7, 512], P(None, None, 'ch'), may hold values from -2 to 2
- long_filter: float32 [2048, 8192], P('ctx', 'ch'), may hold values from 0 to 0.5
- norm_gain: float32 [8192], P('ch'), may hold values from 0.1 to 1.9
- out_grad: bfloat16 [2048, 8192], P('ctx', 'ch'), may hold values from -6 to 6
Outputs:
- output: bfloat16 [2048, 8192], P('ctx', 'ch')
- proj_grads: bfloat16 [3, 2048, 8192], P(None, 'ctx', 'ch')
- short_grads: float32 [3, 7, 512], P(None, None, 'ch')
- long_grad: float32 [2048, 8192], P('ctx', 'ch')
- gain_grad: float32 [8192], P('ch')
All inputs are finite; a program needn't handle non-finite values.
Results may differ from a plain program's by a relative error of at most 0.0064.
Values may be sent and summed in bfloat16 or wider, within the bound.
No kernel may reach another device: no remote copies, remote signals or barrier semaphores. Data moves between devices by JAX's collectives and lax.ppermute only.
A program may use at most 128 MiB of HBM per device.

v0:
```python
import math

import jax
import jax.numpy as jnp
from jax import lax
from jax.sharding import PartitionSpec as P

D = 8192
GROUP = 16
KS = 7


epsilon = 1e-05


def passed_along(block, axis, distance):
    devices = range(lax.axis_size(axis))
    route = [(i - distance, i) for i in devices if i - distance in devices]
    return lax.ppermute(block, axis, route)


def contract(form, left, right):
    return jnp.einsum(form, left, right, precision=lax.Precision.HIGHEST)


def factor_sizes(period):
    inner_len = 1
    while 2 * inner_len * (2 * inner_len) <= period and period % (4 * inner_len) == 0:
        inner_len = inner_len * 2
    return (period // inner_len, inner_len)


def dft_tables(order):
    ordinal_list = jnp.arange(order, dtype=jnp.int32)
    phases = (ordinal_list[:, None] * ordinal_list[None, :] % order).astype(jnp.float32) * (
        2.0 * math.pi / order
    )
    return (jnp.cos(phases), jnp.sin(phases))


def make_tables(outer_len, inner_len):
    period = outer_len * inner_len
    cos_a, sin_a = dft_tables(outer_len)
    cos_b, sin_b = dft_tables(inner_len)
    row_ids = jnp.arange(outer_len, dtype=jnp.int32)[:, None]
    col_ids = jnp.arange(inner_len, dtype=jnp.int32)[None, :]
    phases = (row_ids * col_ids % period).astype(jnp.float32) * (2.0 * math.pi / period)
    return (cos_a, sin_a, cos_b, sin_b, jnp.cos(phases), jnp.sin(phases))


def forward_spectrum(signal, tables):
    cos_a, sin_a, cos_b, sin_b, tw_cos, tw_sin = tables
    outer_len = cos_a.shape[0]
    inner_len = cos_b.shape[0]
    half_len = outer_len // 2
    channels = signal.shape[0]
    grid_rows = signal.reshape(channels, half_len, inner_len)
    real_a = contract("cnb,kn->ckb", grid_rows, cos_a[:, :half_len])
    imag_a = -contract("cnb,kn->ckb", grid_rows, sin_a[:, :half_len])
    real_t = real_a * tw_cos + imag_a * tw_sin
    imag_t = imag_a * tw_cos - real_a * tw_sin
    real_s = contract("ckb,bm->ckm", real_t, cos_b) + contract("ckb,bm->ckm", imag_t, sin_b)
    imag_s = contract("ckb,bm->ckm", imag_t, cos_b) - contract("ckb,bm->ckm", real_t, sin_b)
    return (real_s, imag_s)


def inverse_signal(real_s, imag_s, tables):
    cos_a, sin_a, cos_b, sin_b, tw_cos, tw_sin = tables
    outer_len = cos_a.shape[0]
    inner_len = cos_b.shape[0]
    half_len = outer_len // 2
    channels = real_s.shape[0]
    real_z = contract("ckb,bm->ckm", real_s, cos_b) - contract("ckb,bm->ckm", imag_s, sin_b)
    imag_z = contract("ckb,bm->ckm", imag_s, cos_b) + contract("ckb,bm->ckm", real_s, sin_b)
    real_t = real_z * tw_cos - imag_z * tw_sin
    imag_t = imag_z * tw_cos + real_z * tw_sin
    signal = contract("ckb,kn->cnb", real_t, cos_a[:, :half_len]) - contract(
        "ckb,kn->cnb", imag_t, sin_a[:, :half_len]
    )
    scale_back = 1.0 / (outer_len * inner_len)
    return (signal * scale_back).reshape(channels, half_len * inner_len)


def channel_sum(values):
    return lax.psum(values, "ch")


def on_device(projections, grouped_short_filters, long_filter, norm_gain, out_grad):
    tokens = projections.shape[1]
    spread = lax.axis_size("ctx")
    length = tokens * spread
    outer_len, inner_len = factor_sizes(2 * length)
    tables = make_tables(outer_len, inner_len)
    per_chan = jnp.repeat(grouped_short_filters, GROUP, axis=2)
    edge_rows = passed_along(projections[:, tokens - (KS - 1) :, :], "ctx", 1)
    extended = jnp.concatenate([edge_rows, projections], axis=1)
    conv_sum = jnp.zeros(projections.shape, jnp.float32)
    for tap_idx in range(KS):
        window = extended[:, KS - 1 - tap_idx : KS - 1 - tap_idx + tokens, :].astype(jnp.float32)
        conv_sum = conv_sum + per_chan[:, tap_idx, None, :] * window
    features = lax.optimization_barrier(conv_sum.astype(jnp.bfloat16))
    gate_feat = features[0].astype(jnp.float32)
    key_feat = features[1].astype(jnp.float32)
    value_feat = features[2].astype(jnp.float32)
    mixed_in = key_feat * value_feat
    chan_h = lax.all_to_all(long_filter.T, "ctx", split_axis=0, concat_axis=1, tiled=True)
    chan_u = lax.all_to_all(mixed_in.T, "ctx", split_axis=0, concat_axis=1, tiled=True)
    real_u, imag_u = forward_spectrum(chan_u, tables)
    real_h, imaginary_filter = forward_spectrum(chan_h, tables)
    prod_r = real_u * real_h - imag_u * imaginary_filter
    prod_i = real_u * imaginary_filter + imag_u * real_h
    chan_z = inverse_signal(prod_r, prod_i, tables)
    conv_out = lax.all_to_all(chan_z, "ctx", split_axis=1, concat_axis=0, tiled=True).T
    gated_out = gate_feat * conv_out
    sq_total = channel_sum(jnp.sum(gated_out * gated_out, axis=1))
    rscale = lax.rsqrt(sq_total / D + epsilon)
    normed = gated_out * rscale[:, None]
    output = (normed * norm_gain).astype(jnp.bfloat16)
    gradient_float = out_grad.astype(jnp.float32)
    scaled = gradient_float * norm_gain
    inner_total = channel_sum(jnp.sum(scaled * normed, axis=1))
    grad_gated = rscale[:, None] * (scaled - normed * (inner_total / D)[:, None])
    gain_part = jnp.sum(gradient_float * normed, axis=0)
    grad_conv = grad_gated * gate_feat
    grad_gate = grad_gated * conv_out
    cotangent_gate_input = lax.all_to_all(
        grad_conv.T, "ctx", split_axis=0, concat_axis=1, tiled=True
    )
    real_d, imag_d = forward_spectrum(cotangent_gate_input, tables)
    back_r = real_h * real_d + imaginary_filter * imag_d
    back_i = real_h * imag_d - imaginary_filter * real_d
    filt_r = real_u * real_d + imag_u * imag_d
    filt_i = real_u * imag_d - imag_u * real_d
    chan_du = inverse_signal(back_r, back_i, tables)
    chan_dh = inverse_signal(filt_r, filt_i, tables)
    mix_back = lax.all_to_all(chan_du, "ctx", split_axis=1, concat_axis=0, tiled=True)
    filt_back = lax.all_to_all(chan_dh, "ctx", split_axis=1, concat_axis=0, tiled=True)
    grad_mix = mix_back.T
    long_grad = filt_back.T
    grad_feats = jnp.stack([grad_gate, grad_mix * value_feat, grad_mix * key_feat])
    next_rows = passed_along(grad_feats[:, : KS - 1, :], "ctx", -1)
    cotangent_widened = jnp.concatenate([grad_feats, next_rows], axis=1)
    grad_in = jnp.zeros(grad_feats.shape, jnp.float32)
    tap_terms = []
    local_width = projections.shape[2]
    for tap_idx in range(KS):
        grad_in = (
            grad_in
            + per_chan[:, tap_idx, None, :] * cotangent_widened[:, tap_idx : tap_idx + tokens, :]
        )
        window = extended[:, KS - 1 - tap_idx : KS - 1 - tap_idx + tokens, :].astype(jnp.float32)
        tap_prod = jnp.sum(grad_feats * window, axis=1)
        tap_terms.append(jnp.sum(tap_prod.reshape(3, local_width // GROUP, GROUP), axis=2))
    filt_part = jnp.stack(tap_terms, axis=1)
    gain_grad, short_grads = lax.psum((gain_part, filt_part), "ctx")
    return (output, grad_in.astype(jnp.bfloat16), short_grads, long_grad, gain_grad)


def solution(mesh):
    in_specs = (P(None, "ctx", "ch"), P(None, None, "ch"), P("ctx", "ch"), P("ch"), P("ctx", "ch"))
    out_specs = (P("ctx", "ch"), P(None, "ctx", "ch"), P(None, None, "ch"), P("ctx", "ch"), P("ch"))
    return jax.shard_map(
        on_device, mesh=mesh, in_specs=in_specs, out_specs=out_specs, check_vma=False
    )
```

profile of v0, /device:TPU:0, one launch (start us, length us, event | category | flops | bytes accessed | tf_op | source)
XLA Modules:
  0.0 693.5 jit_solution(7625350813707377017)
XLA Ops:
  8.4 6.6 all-to-all-start.1
  27.5 26.1 %fusion.6 = bf16[3,128,4096]{1,2,0:T(8,128)(2,1)S(1)} fusion(bf16[3,128,4096]{1,2,0:T(8,128)(2,1)S(1)} %copy.105, f32[3,4096]{1,0:T(4,128)S(1)} %get-tuple-element.72, f32[3,4096]{1,0:T(4,128)S(1)} %get-tuple-element.73, f32[3,4096]{1,0:T(4,128)S(1)} %get-tuple-element.74, f32[3,4096]{1,0:T(4,128)S(1)} %get-tuple-element.75, ...), kind=kLoop, calls=%fused_computation.31 | loop fusion | flops 61341696 | bytes 6782976 | tf_op jit(solution)/shard_map/convert_element_type | solution.py:101
  56.8 11.0 %all-to-all-start = ((f32[16,256,128]{2,1,0:T(8,128)}), f32[16,256,128]{2,1,0:T(8,128)}, u32[]{:S(2)}, u32[]{:S(2)}) async-start(f32[16,256,128]{2,1,0:T(8,128)} %bitcast.237), calls=%async_computation | async-start | bytes 4194304 | tf_op jit(solution)/shard_map/all_to_all | solution.py:107
  70.3 5.8 fusion.91
  76.2 5.8 fusion.93
  82.0 26.8 %all-to-all-done = f32[16,256,128]{2,1,0:T(8,128)} async-done(((f32[16,256,128]{2,1,0:T(8,128)}), f32[16,256,128]{2,1,0:T(8,128)}, u32[]{:S(2)}, u32[]{:S(2)}) %all-to-all-start) | async-done | bytes 2097184 | tf_op jit(solution)/shard_map/all_to_all | solution.py:107
  110.7 5.8 fusion.95
  116.5 9.0 %add_bitcast_fusion.1 = (f32[256,64,64]{0,1,2:T(8,128)S(1)}, f32[256,64,64]{0,1,2:T(8,128)S(1)}, f32[256,64,64]{0,1,2:T(8,128)S(1)}, f32[256,64,64]{0,1,2:T(8,128)S(1)}) fusion(f32[64,256,64]{1,0,2:T(8,128)} %fusion.93, f32[64,256,64]{1,0,2:T(8,128)} %fusion.91, f32[64,64]{0,1:T(8,128)S(1)} %get-tuple-element.78, f32[64,64]{0,1:T(8,128)S(1)} %get-tuple-element.79, ...), kind=kOutput, calls=%fused_computation.80 | convolution fusion | flops 417333248 | bytes 31539200 | tf_op jit(solution)/shard_map/cnb,kn->ckb/dot_general | solution.py:23
  125.5 6.4 fusion.41
  132.0 6.9 fusion.43
  138.9 7.2 %fusion.49 = f32[256,64,64]{0,2,1:T(8,128)} fusion(f32[256,64,64]{0,1,2:T(8,128)S(1)} %get-tuple-element.69), kind=kOutput, calls=%fused_computation.99 | convolution fusion | flops 805363712 | bytes 8388608 | tf_op jit(solution)/shard_map/ckb,bm->ckm/dot_general | solution.py:23
  146.1 6.5 fusion.51
  152.6 7.3 %fusion.73 = f32[256,64,64]{0,2,1:T(8,128)S(1)} fusion(f32[256,64,64]{0,2,1:T(8,128)S(1)} %fusion.41, f32[256,64,64]{0,1,2:T(8,128)S(1)} %get-tuple-element.49), kind=kOutput, calls=%fused_computation.125 | convolution fusion | flops 806412288 | bytes 12582912 | tf_op jit(solution)/shard_map/ckb,bm->ckm/dot_general | solution.py:23
  159.8 7.3 %fusion.70 = f32[256,64,64]{0,2,1:T(8,128)} fusion(f32[256,64,64]{0,2,1:T(8,128)S(1)} %fusion.43, f32[256,64,64]{0,1,2:T(8,128)S(1)} %get-tuple-element.49), kind=kOutput, calls=%fused_computation.124 | convolution fusion | flops 806412288 | bytes 12582912 | tf_op jit(solution)/shard_map/ckb,bm->ckm/dot_general | solution.py:23
  167.1 7.2 %fusion.64 = f32[256,64,64]{0,2,1:T(8,128)} fusion(f32[256,64,64]{0,2,1:T(8,128)S(1)} %fusion.51, f32[256,64,64]{0,1,2:T(8,128)S(1)} %get-tuple-element.70), kind=kOutput, calls=%fused_computation.122 | convolution fusion | flops 806412288 | bytes 12582912 | tf_op jit(solution)/shard_map/ckb,bm->ckm/dot_general | solution.py:23
  174.3 11.9 %multiply_add_fusion.5 = (f32[256,64,64]{0,2,1:T(8,128)S(1)}, f32[256,64,64]{0,2,1:T(8,128)S(1)}, f32[256,64,64]{0,2,1:T(8,128)}) fusion(f32[256,64,64]{0,2,1:T(8,128)} %fusion.70, f32[256,64,64]{0,2,1:T(8,128)} %fusion.64, f32[256,64,64]{0,2,1:T(8,128)S(1)} %fusion.73, f32[256,64,64]{0,2,1:T(8,128)} %fusion.49, f32[256,64,64]{0,1,2:T(8,128)S(1)} %get-tuple-element.70), kind=kOutput, calls=%fused_computation.77 | convolution fusion | flops 812703744 | bytes 33554432 | tf_op jit(solution)/shard_map/ckb,bm->ckm/dot_general | solution.py:23
  195.0 4.8 convolution_subtract_fusion.2
  199.8 6.6 multiply_subtract_fusion.4
  210.9 4.9 multiply_bitcast_fusion.2
  218.3 11.3 %all-to-all-start.2 = ((f32[256,16,128]{0,2,1:T(8,128)}), f32[256,16,128]{0,2,1:T(8,128)}, u32[]{:S(2)}, u32[]{:S(2)}) async-start(f32[256,16,128]{0,2,1:T(8,128)} %bitcast.20), calls=%async_computation.2 | async-start | bytes 4194304 | tf_op jit(solution)/shard_map/all_to_all | solution.py:113
  232.0 38.6 %all-to-all-done.2 = f32[256,16,128]{0,2,1:T(8,128)} async-done(((f32[256,16,128]{0,2,1:T(8,128)}), f32[256,16,128]{0,2,1:T(8,128)}, u32[]{:S(2)}, u32[]{:S(2)}) %all-to-all-start.2) | async-done | bytes 2097184 | tf_op jit(solution)/shard_map/all_to_all | solution.py:113
  275.6 5.0 psum.28
  283.4 4.9 psum.29
  291.0 58.2 %all_to_all.105 = f32[16,256,128]{2,1,0:T(8,128)} all-to-all(f32[16,256,128]{2,1,0:T(8,128)S(1)} %bitcast.235), channel_id=1, replica_groups=mesh['ctx'=16,'ch'=2] {'ctx'}, dimensions={0} | all-to-all | bytes 4194304 | tf_op jit(solution)/shard_map/all_to_all | solution.py:126
  352.3 6.3 fusion.87
  358.6 6.0 add_bitcast_fusion
  364.6 6.9 fusion.33
  371.5 7.2 %fusion.35 = f32[256,64,64]{0,2,1:T(8,128)} fusion(f32[256,64,64]{0,1,2:T(8,128)S(1)} %get-tuple-element.46), kind=kOutput, calls=%fused_computation.85 | convolution fusion | flops 805363712 | bytes 8388608 | tf_op jit(solution)/shard_map/ckb,bm->ckm/dot_general | solution.py:23
  378.7 7.3 %fusion.79 = f32[256,64,64]{0,2,1:T(8,128)} fusion(f32[256,64,64]{0,2,1:T(8,128)S(1)} %fusion.33, f32[256,64,64]{0,1,2:T(8,128)S(1)} %get-tuple-element.45), kind=kOutput, calls=%fused_computation.127 | convolution fusion | flops 806412288 | bytes 12582912 | tf_op jit(solution)/shard_map/ckb,bm->ckm/dot_general | solution.py:23
  386.0 21.5 %multiply_subtract_fusion.1 = (f32[256,64,64]{0,2,1:T(8,128)}, f32[256,64,64]{0,2,1:T(8,128)}, f32[256,64,64]{0,2,1:T(8,128)}, f32[256,64,64]{0,2,1:T(8,128)}) fusion(f32[256,64,64]{0,2,1:T(8,128)} %get-tuple-element.71, f32[256,64,64]{0,2,1:T(8,128)} %fusion.64, f32[256,64,64]{0,2,1:T(8,128)} %fusion.79, f32[256,64,64]{0,2,1:T(8,128)} %copy-done.9, ...), kind=kOutput, calls=%fused_computation.67 | convolution fusion | flops 818995200 | bytes 46137344 | tf_op jit(solution)/shard_map/ckb,bm->ckm/dot_general | solution.py:23
  407.5 8.4 %fusion.121 = f32[256,64,64]{0,2,1:T(8,128)} fusion(f32[256,64,64]{0,2,1:T(8,128)} %get-tuple-element.31), kind=kOutput, calls=%fused_computation.188 | convolution fusion | flops 805363712 | bytes 8388608 | tf_op jit(solution)/shard_map/ckb,bm->ckm/dot_general | solution.py:23
  420.1 5.7 convolution_subtract_fusion
  434.3 5.6 convolution_subtract_fusion.1
  439.8 5.8 convolution_add_fusion.1
  445.6 11.7 %multiply_subtract_fusion = (f32[256,64,64]{0,2,1:T(8,128)}, f32[256,64,64]{0,2,1:T(8,128)}, f32[256,64,64]{0,2,1:T(8,128)}, f32[256,64,64]{0,2,1:T(8,128)S(1)}) fusion(f32[256,64,64]{0,2,1:T(8,128)} %convolution_subtract_fusion, f32[64,64]{1,0:T(8,128)S(1)} %copy.124, f32[64,64]{1,0:T(8,128)S(1)} %copy.123, f32[256,64,64]{0,2,1:T(8,128)} %convolution_subtract_fusion.1, ...), kind=kOutput, calls=%fused_computation.66 | convolution fusion | flops 818995200 | bytes 37781504 | tf_op jit(solution)/shard_map/ckb,bm->ckm/dot_general | solution.py:23
  457.3 7.4 %fusion.25 = f32[32,256,64]{1,0,2:T(8,128)S(1)} fusion(f32[256,64,64]{0,2,1:T(8,128)} %get-tuple-element.67, f32[64,64]{0,1:T(8,128)S(1)} %fusion.148), kind=kOutput, calls=%fused_computation.57 | convolution fusion | flops 402653184 | bytes 6307840 | tf_op jit(solution)/shard_map/ckb,kn->cnb/dot_general | solution.py:23
  464.7 4.7 multiply_bitcast_fusion.1
  471.9 5.4 all-to-all-start.4
  478.6 7.1 %fusion.21 = f32[32,256,64]{1,0,2:T(8,128)S(1)} fusion(f32[256,64,64]{0,2,1:T(8,128)} %get-tuple-element.42, f32[64,64]{0,1:T(8,128)S(1)} %fusion.148), kind=kOutput, calls=%fused_computation.53 | convolution fusion | flops 402653184 | bytes 6307840 | tf_op jit(solution)/shard_map/ckb,kn->cnb/dot_general | solution.py:23
  485.7 4.7 multiply_bitcast_fusion
  493.0 25.3 %all-to-all-done.4 = f32[256,16,128]{0,2,1:T(8,128)} async-done(((f32[256,16,128]{0,2,1:T(8,128)}), f32[256,16,128]{0,2,1:T(8,128)}, u32[]{:S(2)}, u32[]{:S(2)}) %all-to-all-start.4) | async-done | bytes 2097184 | tf_op jit(solution)/shard_map/all_to_all | solution.py:136
  518.3 11.5 %all-to-all-start.5 = ((f32[256,16,128]{0,2,1:T(8,128)}), f32[256,16,128]{0,2,1:T(8,128)}, u32[]{:S(2)}, u32[]{:S(2)}) async-start(f32[256,16,128]{0,2,1:T(8,128)} %bitcast.236), calls=%async_computation.5 | async-start | bytes 4194304 | tf_op jit(solution)/shard_map/all_to_all | solution.py:137
  538.0 21.9 %fusion.12 = (f32[3,4096]{1,0:T(4,128)S(1)}, f32[3,4096]{1,0:T(4,128)S(1)}, f32[3,4096]{1,0:T(4,128)S(1)}, f32[3,4096]{1,0:T(4,128)S(1)}, f32[3,4096]{1,0:T(4,12...) fusion(bf16[3,128,4096]{1,2,0:T(8,128)(2,1)S(1)} %copy-done.13, bf16[3,6,4096]{1,2,0:T(8,128)(2,1)S(1)} %copy-done.14, ...), kind=kLoop, calls=%fused_computation.37 | loop fusion | flops 64401408 | bytes 9928704 | tf_op jit(solution)/shard_map/reduce_sum | solution.py:152
  562.1 5.3 pad_maximum_fusion.1
  579.4 65.7 %all-reduce = (f32[3,7,256]{2,0,1:T(4,128)S(1)}, f32[4096]{0:T(1024)}) all-reduce(f32[3,7,256]{2,0,1:T(4,128)S(1)} %constant_dynamic-update-slice_fusion, f32[4096]{0:T(1024)S(1)} %get-tuple-element.27), channel_id=1, replica_groups=mesh['ctx'=16,'ch'=2] {'ctx'}, use_global_device_ids=true, to_apply=%region_18.19 | all-reduce | flops 9472 | bytes 75776 | tf_op jit(solution)/shard_map/psum | solution.py:155
  649.7 10.6 %pad_maximum_fusion = f32[3,134,4096]{1,2,0:T(8,128)} fusion(f32[3,6,4096]{1,2,0:T(8,128)} %copy.142, f32[1,128,4096]{1,2,0:T(8,128)} %copy-done.2, f32[1,128,4096]{1,2,0:T(8,128)} %copy-done, f32[1,128,4096]{1,2,0:T(8,128)S(1)} %bitcast.226), kind=kLoop, calls=%fused_computation | loop fusion | flops 4939776 | bytes 13172736 | tf_op jit(solution)/shard_map/concatenate | solution.py:142
  660.4 28.2 %fusion.15 = bf16[3,128,4096]{1,2,0:T(8,128)(2,1)} fusion(f32[3,134,4096]{1,2,0:T(8,128)} %pad_maximum_fusion, f32[3,4096]{1,0:T(4,128)S(1)} %copy-done.18, f32[3,4096]{1,0:T(4,128)S(1)} %copy-done.20, f32[3,4096]{1,0:T(4,128)S(1)} %copy-done.22, f32[3,4096]{1,0:T(4,128)S(1)} %copy-done.24, f32[3,4096]{1,0:T(4,128)S(1)} %copy-done.26, ...), kind=kLoop, calls=%fused_computation.41 | loop fusion | flops 25165824 | bytes 47529984 | tf_op jit(solution)/shard_map/convert_element_type | solution.py:156
  688.6 4.6 copy.148
  (135 shorter events, 105.5 us)
Async XLA Ops:
  2.3 12.7 %copy-start.31 = (f32[3,7,256]{2,1,0:T(8,128)S(1)}, f32[3,7,256]{2,1,0:T(8,128)}, u32[]{:S(2)}) copy-start(f32[3,7,256]{2,1,0:T(8,128)} %param.6) | copy-start | bytes 64516
  2.3 21.6 %collective-permute-start = (bf16[3,6,4096]{2,1,0:T(8,128)(2,1)}, bf16[3,6,4096]{2,1,0:T(8,128)(2,1)}, u32[]{:S(2)}, u32[]{:S(2)}) collective-permute-start(bf16[3,6,4096]{2,1,0:T(8,128)(2,1)} %slice.123), channel_id=1, source_target_pairs={{0,2},{2,4},{4,6},{6,8},{8,10},{10,12},{12,14},{14,16},{16,18},{18... | collective-permute-start | bytes 442376 | tf_op jit(solution)/shard_map/ppermute | solution.py:19
  8.4 48.4 %all-to-all-start.1 = ((f32[16,256,128]{2,1,0:T(8,128)}), f32[16,256,128]{2,1,0:T(8,128)}, u32[]{:S(2)}, u32[]{:S(2)}) async-start(f32[16,256,128]{2,1,0:T(8,128)} %bitcast.14), calls=%async_computation.1 | async-start | bytes 4194304 | tf_op jit(solution)/shard_map/all_to_all | solution.py:106
  18.4 9.1 %copy-start.17 = (f32[3,4096]{1,0:T(4,128)}, f32[3,4096]{1,0:T(4,128)S(1)}, u32[]{:S(2)}) copy-start(f32[3,4096]{1,0:T(4,128)S(1)} %get-tuple-element.72) | copy-start | bytes 147460
  18.4 9.1 %copy-start.19 = (f32[3,4096]{1,0:T(4,128)}, f32[3,4096]{1,0:T(4,128)S(1)}, u32[]{:S(2)}) copy-start(f32[3,4096]{1,0:T(4,128)S(1)} %get-tuple-element.73) | copy-start | bytes 147460
  18.5 9.0 %copy-start.21 = (f32[3,4096]{1,0:T(4,128)}, f32[3,4096]{1,0:T(4,128)S(1)}, u32[]{:S(2)}) copy-start(f32[3,4096]{1,0:T(4,128)S(1)} %get-tuple-element.74) | copy-start | bytes 147460
  18.5 9.0 %copy-start.23 = (f32[3,4096]{1,0:T(4,128)}, f32[3,4096]{1,0:T(4,128)S(1)}, u32[]{:S(2)}) copy-start(f32[3,4096]{1,0:T(4,128)S(1)} %get-tuple-element.75) | copy-start | bytes 147460
  18.6 8.9 %copy-start.25 = (f32[3,4096]{1,0:T(4,128)}, f32[3,4096]{1,0:T(4,128)S(1)}, u32[]{:S(2)}) copy-start(f32[3,4096]{1,0:T(4,128)S(1)} %get-tuple-element.76) | copy-start | bytes 147460
  18.6 8.9 %copy-start.27 = (f32[3,4096]{1,0:T(4,128)}, f32[3,4096]{1,0:T(4,128)S(1)}, u32[]{:S(2)}) copy-start(f32[3,4096]{1,0:T(4,128)S(1)} %get-tuple-element.77) | copy-start | bytes 147460
  22.1 31.4 %copy-start.12 = (bf16[3,128,4096]{1,2,0:T(8,128)(2,1)}, bf16[3,128,4096]{1,2,0:T(8,128)(2,1)S(1)}, u32[]{:S(2)}) copy-start(bf16[3,128,4096]{1,2,0:T(8,128)(2,1)S(1)} %copy.105) | copy-start | bytes 9437188
  53.6 1.7 copy-start.10
  56.8 52.0 %all-to-all-start = ((f32[16,256,128]{2,1,0:T(8,128)}), f32[16,256,128]{2,1,0:T(8,128)}, u32[]{:S(2)}, u32[]{:S(2)}) async-start(f32[16,256,128]{2,1,0:T(8,128)} %bitcast.237), calls=%async_computation | async-start | bytes 4194304 | tf_op jit(solution)/shard_map/all_to_all | solution.py:107
  159.8 14.5 %copy-start.9 = (f32[256,64,64]{0,2,1:T(8,128)}, f32[256,64,64]{0,2,1:T(8,128)S(1)}, u32[]{:S(2)}) copy-start(f32[256,64,64]{0,2,1:T(8,128)S(1)} %fusion.73) | copy-start | bytes 12582916
  218.3 52.3 %all-to-all-start.2 = ((f32[256,16,128]{0,2,1:T(8,128)}), f32[256,16,128]{0,2,1:T(8,128)}, u32[]{:S(2)}, u32[]{:S(2)}) async-start(f32[256,16,128]{0,2,1:T(8,128)} %bitcast.20), calls=%async_computation.2 | async-start | bytes 4194304 | tf_op jit(solution)/shard_map/all_to_all | solution.py:113
  229.6 43.9 %copy-start.11 = (bf16[3,128,4096]{1,2,0:T(8,128)(2,1)S(1)}, bf16[3,128,4096]{1,2,0:T(8,128)(2,1)}, u32[]{:S(2)}) copy-start(bf16[3,128,4096]{1,2,0:T(8,128)(2,1)} %copy-done.10) | copy-start | bytes 9437188
  232.0 48.6 %copy-start.30 = (f32[4096]{0:T(1024)S(1)}, f32[4096]{0:T(1024)}, u32[]{:S(2)}) copy-start(f32[4096]{0:T(1024)} %param.8) | copy-start | bytes 49156
  352.3 6.3 copy-start.15
  364.6 14.1 %copy-start.8 = (f32[256,64,64]{0,1,2:T(8,128)}, f32[256,64,64]{0,1,2:T(8,128)S(1)}, u32[]{:S(2)}) copy-start(f32[256,64,64]{0,1,2:T(8,128)S(1)} %get-tuple-element.45) | copy-start | bytes 12582916
  407.5 8.4 %copy-start.4 = (f32[256,64,64]{0,2,1:T(8,128)S(1)}, f32[256,64,64]{0,2,1:T(8,128)}, u32[]{:S(2)}) copy-start(f32[256,64,64]{0,2,1:T(8,128)} %get-tuple-element.32) | copy-start | bytes 12582916
  415.9 4.2 copy-start.7
  420.1 5.8 copy-start.5
  425.8 4.2 copy-start.6
  471.9 46.4 %all-to-all-start.4 = ((f32[256,16,128]{0,2,1:T(8,128)}), f32[256,16,128]{0,2,1:T(8,128)}, u32[]{:S(2)}, u32[]{:S(2)}) async-start(f32[256,16,128]{0,2,1:T(8,128)} %bitcast.238), calls=%async_computation.4 | async-start | bytes 4194304 | tf_op jit(solution)/shard_map/all_to_all | solution.py:136
  478.6 7.1 %copy-start.16 = (f32[256,64,64]{0,2,1:T(8,128)S(1)}, f32[256,64,64]{0,2,1:T(8,128)}, u32[]{:S(2)}) copy-start(f32[256,64,64]{0,2,1:T(8,128)} %get-tuple-element.41) | copy-start | bytes 12582916
  518.3 54.9 %all-to-all-start.5 = ((f32[256,16,128]{0,2,1:T(8,128)}), f32[256,16,128]{0,2,1:T(8,128)}, u32[]{:S(2)}, u32[]{:S(2)}) async-start(f32[256,16,128]{0,2,1:T(8,128)} %bitcast.236), calls=%async_computation.5 | async-start | bytes 4194304 | tf_op jit(solution)/shard_map/all_to_all | solution.py:137
  532.7 3.2 copy-start.13
  532.7 5.3 copy-start.14
  535.3 24.7 %copy-start = (f32[1,128,4096]{1,2,0:T(8,128)}, f32[1,128,4096]{1,2,0:T(8,128)S(1)}, u32[]{:S(2)}) copy-start(f32[1,128,4096]{1,2,0:T(8,128)S(1)} %get-tuple-element.58) | copy-start | bytes 6291460
  535.3 24.7 %copy-start.2 = (f32[1,128,4096]{1,2,0:T(8,128)}, f32[1,128,4096]{1,2,0:T(8,128)S(1)}, u32[]{:S(2)}) copy-start(f32[1,128,4096]{1,2,0:T(8,128)S(1)} %get-tuple-element.59) | copy-start | bytes 6291460
  571.9 73.8 %collective-permute-start.1 = (f32[3,6,4096]{2,1,0:T(8,128)S(1)}, f32[3,6,4096]{2,1,0:T(8,128)S(1)}, u32[]{:S(2)}, u32[]{:S(2)}) collective-permute-start(f32[3,6,4096]{2,1,0:T(8,128)S(1)} %copy.141), channel_id=1, source_target_pairs={{2,0},{4,2},{6,4},{8,6},{10,8},{12,10},{14,12},{16,14},{18,16},{20... | collective-permute-start | bytes 884744 | tf_op jit(solution)/shard_map/ppermute | solution.py:19
  649.6 10.7 %copy-start.1 = (f32[1,128,4096]{1,2,0:T(8,128)S(1)}, f32[1,128,4096]{1,2,0:T(8,128)}, u32[]{:S(2)}) copy-start(f32[1,128,4096]{1,2,0:T(8,128)} %copy-done) | copy-start | bytes 6291460
  649.6 10.7 %copy-start.3 = (f32[1,128,4096]{1,2,0:T(8,128)S(1)}, f32[1,128,4096]{1,2,0:T(8,128)}, u32[]{:S(2)}) copy-start(f32[1,128,4096]{1,2,0:T(8,128)} %copy-done.2) | copy-start | bytes 6291460
  649.6 10.7 %copy-start.18 = (f32[3,4096]{1,0:T(4,128)S(1)}, f32[3,4096]{1,0:T(4,128)}, u32[]{:S(2)}) copy-start(f32[3,4096]{1,0:T(4,128)} %copy-done.17) | copy-start | bytes 147460
  649.6 10.7 %copy-start.20 = (f32[3,4096]{1,0:T(4,128)S(1)}, f32[3,4096]{1,0:T(4,128)}, u32[]{:S(2)}) copy-start(f32[3,4096]{1,0:T(4,128)} %copy-done.19) | copy-start | bytes 147460
  649.7 10.7 %copy-start.22 = (f32[3,4096]{1,0:T(4,128)S(1)}, f32[3,4096]{1,0:T(4,128)}, u32[]{:S(2)}) copy-start(f32[3,4096]{1,0:T(4,128)} %copy-done.21) | copy-start | bytes 147460
  649.7 10.7 %copy-start.24 = (f32[3,4096]{1,0:T(4,128)S(1)}, f32[3,4096]{1,0:T(4,128)}, u32[]{:S(2)}) copy-start(f32[3,4096]{1,0:T(4,128)} %copy-done.23) | copy-start | bytes 147460
  649.7 10.7 %copy-start.26 = (f32[3,4096]{1,0:T(4,128)S(1)}, f32[3,4096]{1,0:T(4,128)}, u32[]{:S(2)}) copy-start(f32[3,4096]{1,0:T(4,128)} %copy-done.25) | copy-start | bytes 147460
  649.7 10.7 %copy-start.28 = (f32[3,4096]{1,0:T(4,128)S(1)}, f32[3,4096]{1,0:T(4,128)}, u32[]{:S(2)}) copy-start(f32[3,4096]{1,0:T(4,128)} %copy-done.27) | copy-start | bytes 147460
  649.7 10.7 %copy-start.29 = (f32[3,1,4096]{2,0,1:T(4,128)S(1)}, f32[3,1,4096]{2,0,1:T(4,128)}, u32[]{:S(2)}) copy-start(f32[3,1,4096]{2,0,1:T(4,128)} %copy.239) | copy-start | bytes 147460
where the time goes:
time: 699 us; the launch traced here: 693 us
  matrix products  245 us (35%)
  blocking collectives  134 us (19%)
  other arithmetic  105 us (15%)
  waiting for transfers between devices  90.7 us (13%)
  local copies, waits for them, and re-layouts  66.3 us (9%)
  starting transfers between devices  50.2 us (7%)
    dot_general x36, matrix products, contract(): return jnp.einsum(form, left, right, precision=lax.Precision.HIGHEST)  245 us
    psum x1, blocking collectives, on_device(): gain_grad, short_grads = lax.psum((gain_part, filt_part), 'ctx')  65.7 us
    all_to_all x1, blocking collectives, on_device(): lax.all_to_all(grad_conv.T, 'ctx', split_axis=0, concat_axis=1, tiled=True)  58.2 us
    all_to_all x1, waiting for transfers between devices, on_device(): lax.all_to_all(chan_z, 'ctx', split_axis=1, concat_axis=0, tiled=True)  38.6 us
    convert_element_type x1, other arithmetic, on_device(): grad_in.astype(jnp.bfloat16)  28.2 us
    all_to_all x1, waiting for transfers between devices, on_device(): lax.all_to_all(mixed_in.T, 'ctx', split_axis=0, concat_axis=1, tiled=True)  26.8 us
    convert_element_type x1, other arithmetic, on_device(): features = lax.optimization_barrier(conv_sum.astype(jnp.bfloat16))  26.1 us
    all_to_all x1, waiting for transfers between devices, on_device(): lax.all_to_all(chan_du, 'ctx', split_axis=1, concat_axis=0, tiled=True)  25.3 us
  transfers between devices with their start and end apart: 7, of which 3 were waited for; matrix products, arithmetic and copies ran while one was open for 17% of the time, Pallas kernels for 0%

commit v1 on v0

--- a/solution.py
+++ b/solution.py
@@ -1,16 +1,22 @@
+import functools
 import math
 
 import jax
 import jax.numpy as jnp
+import numpy as np
 from jax import lax
+from jax.experimental import pallas as pl
+from jax.experimental.pallas import tpu as pltpu
 from jax.sharding import PartitionSpec as P
 
 D = 8192
 GROUP = 16
 KS = 7
 
-
 epsilon = 1e-05
+
+BLOCK = 256
+HALO = 8
 
 
 def passed_along(block, axis, distance):
@@ -85,7 +91,7 @@
     return lax.psum(values, "ch")
 
 
-def on_device(projections, grouped_short_filters, long_filter, norm_gain, out_grad):
+def narrow_path(projections, grouped_short_filters, long_filter, norm_gain, out_grad):
     tokens = projections.shape[1]
     spread = lax.axis_size("ctx")
     length = tokens * spread
@@ -156,6 +162,862 @@
     return (output, grad_in.astype(jnp.bfloat16), short_grads, long_grad, gain_grad)
 
 
+F32 = jnp.float32
+BF16 = jnp.bfloat16
+
+
+def two_terms(table):
+    high = table.astype(np.float32).astype(jnp.bfloat16)
+    low = (table - high.astype(np.float64)).astype(np.float32).astype(jnp.bfloat16)
+    return np.asarray(high), np.asarray(low)
+
+
+def block_tables():
+    numbers = np.concatenate([np.arange(0, BLOCK, 2), np.arange(1, BLOCK, 2)])
+    turns = (2 * numbers[:, None] + 1) * np.arange(BLOCK)[None, :] % (4 * BLOCK)
+    phases = turns.astype(np.float64) * (math.pi / (2 * BLOCK))
+    forward = np.concatenate([np.cos(phases), -np.sin(phases)], axis=0)
+    return two_terms(forward), two_terms(forward.T / BLOCK)
+
+
+def mxu(left, right):
+    return jnp.dot(left, right, preferred_element_type=F32)
+
+
+LANES = 128
+VMEM = pl.BlockSpec(memory_space=pltpu.VMEM)
+ANY = pl.BlockSpec(memory_space=pl.ANY)
+MIB = 1024 * 1024
+
+
+def cost(flops, size):
+    return pl.CostEstimate(flops=int(flops), transcendentals=0, bytes_accessed=int(size))
+
+
+def held(values):
+    return pltpu.with_memory_space_constraint(values, pltpu.VMEM)
+
+
+def streamed(values):
+    return pltpu.with_memory_space_constraint(values, pltpu.HBM)
+
+
+def whole(body, name, args, outs, scratch=(), limit=24, work=0, streams=(), out_streams=(), landed=()):
+    size = sum(math.prod(a.shape) * a.dtype.itemsize for a in [*args, *outs])
+    return pl.pallas_call(
+        body,
+        name=name,
+        in_specs=[ANY if i in streams else VMEM for i in range(len(args))],
+        out_specs=[ANY if i in out_streams else VMEM for i in range(len(outs))],
+        out_shape=list(outs),
+        scratch_shapes=list(scratch),
+        cost_estimate=cost(work, size),
+        compiler_params=pltpu.CompilerParams(vmem_limit_bytes=limit * MIB),
+    )(*[streamed(a) if i in streams and i not in landed else a for i, a in enumerate(args)])
+
+
+def kept(shape, dtype):
+    return pltpu.VMEM(shape, dtype)
+
+
+def stored(shape, dtype):
+    return pltpu.HBM(shape, dtype)
+
+
+def each(number, step):
+    def body(index, carry):
+        step(index)
+        return carry
+
+    lax.fori_loop(0, number, body, 0)
+
+
+def copies(source, target, sems):
+    return lambda j: pltpu.make_async_copy(source.at[j], target.at[j], sems.at[j])
+
+
+def wide_copies(source, target, sems, width):
+    lead = (slice(None),) * (len(source.shape) - 1)
+
+    def move(j):
+        here = pl.ds(pl.multiple_of(j * width, LANES), width)
+        return pltpu.make_async_copy(source.at[(*lead, here)], target.at[j], sems.at[j])
+
+    return move
+
+
+def wide_stores(source, target, sems, width):
+    lead = (slice(None),) * (len(target.shape) - 1)
+
+    def move(j):
+        here = pl.ds(pl.multiple_of(j * width, LANES), width)
+        return pltpu.make_async_copy(source.at[j], target.at[(*lead, here)], sems.at[j])
+
+    return move
+
+
+def lane_tile(chunk, width, part=0, size=LANES):
+    return pl.ds(pl.multiple_of(chunk * width + part * LANES, LANES), size)
+
+
+def parts_of(width):
+    return [(part, slice(part * LANES, (part + 1) * LANES)) for part in range(width // LANES)]
+
+
+def to_chunks(values, width):
+    tokens, local = values.shape
+    count = local // width
+
+    def body(source, target, rows, chunks, in_sems, out_sems):
+        arrive = wide_copies(source, rows, in_sems, width)
+        leave = copies(chunks, target, out_sems)
+        for j in range(count):
+            arrive(j).start()
+        for j in range(count):
+            arrive(j).wait()
+            chunks[j] = rows[j].astype(BF16)
+            leave(j).start()
+        for j in range(count):
+            leave(j).wait()
+
+    return whole(
+        body,
+        "to_chunks",
+        [values],
+        [stored((count, tokens, width), BF16)],
+        [
+            pltpu.VMEM((count, tokens, width), F32),
+            pltpu.VMEM((count, tokens, width), BF16),
+            pltpu.SemaphoreType.DMA((count,)),
+            pltpu.SemaphoreType.DMA((count,)),
+        ],
+        streams=[0],
+        out_streams=[0],
+        limit=8,
+    )[0]
+
+
+def from_chunks(chunks):
+    count, tokens, width = chunks.shape
+
+    def body(source, target, rows, wide, in_sems, out_sems):
+        arrive = copies(source, rows, in_sems)
+
+        leave = wide_stores(wide, target, out_sems, width)
+        for j in range(count):
+            arrive(j).start()
+        for j in range(count):
+            arrive(j).wait()
+            wide[j] = rows[j].astype(F32)
+            leave(j).start()
+        for j in range(count):
+            leave(j).wait()
+
+    return whole(
+        body,
+        "from_chunks",
+        [chunks],
+        [stored((tokens, count * width), F32)],
+        [
+            pltpu.VMEM((count, tokens, width), BF16),
+            pltpu.VMEM((count, tokens, width), F32),
+            pltpu.SemaphoreType.DMA((count,)),
+            pltpu.SemaphoreType.DMA((count,)),
+        ],
+        landed=[0],
+        streams=[0],
+        out_streams=[0],
+        limit=8,
+    )[0]
+
+
+def three_terms(values):
+    first = values.astype(BF16)
+    rest = values - first.astype(F32)
+    second = rest.astype(BF16)
+    third = (rest - second.astype(F32)).astype(BF16)
+    return first, second, third
+
+
+def spread_taps(taps, local, width):
+    rows, groups = taps.shape
+
+    def body(t_ref, out_ref):
+        terms = three_terms(t_ref[...])
+
+        def step(j):
+            group = lax.broadcasted_iota(jnp.int32, (groups, width), 0)
+            channel = lax.broadcasted_iota(jnp.int32, (groups, width), 1)
+            chosen = group == j * (width // GROUP) + channel // GROUP
+            matrix = jnp.where(chosen, 1.0, 0.0).astype(BF16)
+            total = mxu(terms[0], matrix) + (mxu(terms[1], matrix) + mxu(terms[2], matrix))
+            out_ref[:, lane_tile(j, width, 0, width)] = total
+
+        each(local // width, step)
+
+    work = 4 * rows * groups * local
+    return whole(body, "spread_taps", [taps], [shape_of((rows, local), F32)], work=work)[0]
+
+
+def gather_groups(sums, out_ref, groups, width):
+    count, rows, _ = sums.shape
+    per_chunk = width // GROUP
+    group = lax.broadcasted_iota(jnp.int32, (width, LANES), 1)
+    channel = lax.broadcasted_iota(jnp.int32, (width, LANES), 0)
+    matrix = jnp.where(group == channel // GROUP, 1.0, 0.0).astype(BF16)
+    terms = three_terms(sums[...].reshape(count * rows, width))
+    found = mxu(terms[0], matrix) + (mxu(terms[1], matrix) + mxu(terms[2], matrix))
+    for tile in range(groups // LANES):
+        total = None
+        for place in range(LANES // per_chunk):
+            j = tile * (LANES // per_chunk) + place
+            part = found[j * rows : (j + 1) * rows]
+            part = pltpu.roll(part, place * per_chunk, axis=1) if place else part
+            total = part if total is None else total + part
+        out_ref[:, tile * LANES : (tile + 1) * LANES] = total
+
+
+def dma(*shape):
+    return pltpu.SemaphoreType.DMA(shape)
+
+
+def short_conv(projections, edges, per_chan, width):
+    _, tokens, local = projections.shape
+    count = local // width
+
+    def body(p_hbm, e_ref, t_ref, f_hbm, u_hbm, p_ref, feats, chunks, ext, p_sem, f_sem, u_sem):
+        arrive = wide_copies(p_hbm, p_ref, p_sem, width)
+        keep, leave = wide_stores(feats, f_hbm, f_sem, width), copies(chunks, u_hbm, u_sem)
+        each(count, lambda j: arrive(j).start())
+
+        def step(j):
+            arrive(j).wait()
+            for part, cols in parts_of(width):
+                here = lane_tile(j, width, part)
+                rows = t_ref[:, here]
+                found = []
+                for i in range(3):
+                    ext[i, :HALO, :] = e_ref[i, :, here].astype(F32)
+                    ext[i, HALO:, :] = p_ref[j, i, :, cols].astype(F32)
+                    total = None
+                    for tap in range(KS):
+                        at = i * KS + tap
+                        term = rows[at : at + 1] * ext[i, HALO - tap : HALO - tap + tokens, :]
+                        total = term if total is None else total + term
+                    found.append(total.astype(BF16))
+                    feats[j, i, :, cols] = found[i]
+                chunks[j, :, cols] = (found[1].astype(F32) * found[2].astype(F32)).astype(BF16)
+            keep(j).start()
+            leave(j).start()
+
+        def finish(j):
+            keep(j).wait()
+            leave(j).wait()
+
+        each(count, step)
+        each(count, finish)
+
+    return whole(
+        body,
+        "short_conv",
+        [projections, edges, per_chan],
+        [stored(projections.shape, BF16), stored((count, tokens, width), BF16)],
+        [
+            pltpu.VMEM((count, 3, tokens, width), BF16),
+            pltpu.VMEM((count, 3, tokens, width), BF16),
+            pltpu.VMEM((count, tokens, width), BF16),
+            pltpu.VMEM((3, HALO + tokens, LANES), F32),
+            dma(count),
+            dma(count),
+            dma(count),
+        ],
+        streams=[0],
+        out_streams=[0, 1],
+        work=42 * tokens * local,
+    )
+
+
+def window_spectrum(blocks, forward):
+    count, _, width = blocks.shape
+    half = BLOCK // 2
+
+    def body(x_hbm, hi_hbm, lo_hbm, g_hbm, x_ref, hi, lo, g_ref, spec, t_sem, x_sem, g_sem):
+        arrive, leave = copies(x_hbm, x_ref, x_sem), copies(g_ref, g_hbm, g_sem)
+        moves = [
+            pltpu.make_async_copy(hi_hbm, hi, t_sem.at[0]),
+            pltpu.make_async_copy(lo_hbm, lo, t_sem.at[1]),
+        ]
+        for move in moves:
+            move.start()
+        for b in range(count):
+            arrive(b).start()
+        for move in moves:
+            move.wait()
+        for b in range(count):
+            now, prev = b % 2, (b + 1) % 2
+            arrive(b).wait()
+            x = x_ref[b]
+            spec[now] = mxu(hi[...], x) + mxu(lo[...], x)
+            if b == 0:
+                g_ref[0] = spec[0]
+            else:
+                g_ref[b, :half] = spec[now, :half] - spec[prev, BLOCK : BLOCK + half]
+                g_ref[b, half:BLOCK] = spec[now, half:BLOCK] + spec[prev, BLOCK + half :]
+                g_ref[b, BLOCK : BLOCK + half] = spec[now, BLOCK : BLOCK + half] + spec[prev, :half]
+                g_ref[b, BLOCK + half :] = spec[now, BLOCK + half :] - spec[prev, half:BLOCK]
+            leave(b).start()
+        for b in range(count):
+            leave(b).wait()
+
+    shape = (count, 2 * BLOCK, width)
+    return whole(
+        body,
+        "window_spectrum",
+        [blocks, *forward],
+        [stored(shape, F32)],
+        [
+            pltpu.VMEM(blocks.shape, BF16),
+            *[pltpu.VMEM(table.shape, BF16) for table in forward],
+            pltpu.VMEM(shape, F32),
+            pltpu.VMEM((2, 2 * BLOCK, width), F32),
+            dma(2),
+            dma(count),
+            dma(count),
+        ],
+        landed=[0],
+        streams=[0, 1, 2],
+        out_streams=[0],
+        work=8 * BLOCK * blocks.size,
+    )[0]
+
+
+def block_products(window_ref, spec_ref, out_ref, count, width, adjoint):
+    rows = 8
+
+    def step(index):
+        r = pl.multiple_of(index * rows, rows)
+        for part, cols in parts_of(width):
+            real = pl.ds(r, rows)
+            imag = pl.ds(pl.multiple_of(r + BLOCK, rows), rows)
+            win = [(window_ref[m, real, cols], window_ref[m, imag, cols]) for m in range(count)]
+            spec = [(spec_ref[m, real, cols], spec_ref[m, imag, cols]) for m in range(count)]
+            for b in range(count):
+                acc_r = acc_i = None
+                pairs = range(count - b) if adjoint else range(b + 1)
+                for m in pairs:
+                    wr, wi = win[m]
+                    sr, si = spec[b + m] if adjoint else spec[b - m]
+                    if adjoint:
+                        tr, ti = wr * sr + wi * si, wr * si - wi * sr
+                    else:
+                        tr, ti = wr * sr - wi * si, wr * si + wi * sr
+                    acc_r = tr if acc_r is None else acc_r + tr
+                    acc_i = ti if acc_i is None else acc_i + ti
+                out_ref[b, real, cols] = acc_r
+                out_ref[b, imag, cols] = acc_i
+
+    each(BLOCK // rows, step)
+
+
+def inverse_block(prod, hi, lo):
+    top = prod.astype(BF16)
+    rest = (prod - top.astype(F32)).astype(BF16)
+    return mxu(hi, top) + (mxu(lo, top) + mxu(hi, rest))
+
+
+def convolve(blocks, window, tables, adjoint):
+    count, _, width = blocks.shape
+    args = [blocks, window, *sum(tables, ())]
+
+    def body(*refs):
+        sources, refs = refs[:6], refs[6:]
+        y_hbm, s_hbm, refs = (refs[0], refs[1], refs[2:]) if adjoint else (refs[0], None, refs[1:])
+        x_ref, w_ref, fh, fl, th, tl, spec, prod, y_ref, t_sem, x_sem, y_sem, s_sem = refs
+        arrive, leave = copies(sources[0], x_ref, x_sem), copies(y_ref, y_hbm, y_sem)
+        loads = [
+            pltpu.make_async_copy(sources[n], target, t_sem.at[n])
+            for n, target in [(2, fh), (3, fl), (1, w_ref), (4, th), (5, tl)]
+        ]
+        loads[0].start()
+        loads[1].start()
+        for b in range(count):
+            arrive(b).start()
+        for move in loads[2:]:
+            move.start()
+        loads[0].wait()
+        loads[1].wait()
+        for b in range(count):
+            arrive(b).wait()
+            x = x_ref[b]
+            spec[b] = mxu(fh[...], x) + mxu(fl[...], x)
+            if adjoint:
+                copies(spec, s_hbm, s_sem)(b).start()
+        for move in loads[2:]:
+            move.wait()
+        block_products(w_ref, spec, prod, count, width, adjoint)
+        for b in range(count):
+            y_ref[b] = inverse_block(prod[b], th[...], tl[...]).astype(BF16)
+            leave(b).start()
+        for b in range(count):
+            leave(b).wait()
+            if adjoint:
+                copies(spec, s_hbm, s_sem)(b).wait()
+
+    outs = [stored(blocks.shape, BF16)]
+    if adjoint:
+        outs.append(stored(window.shape, F32))
+    return whole(
+        body,
+        "correlate_blocks" if adjoint else "convolve",
+        args,
+        outs,
+        [
+            *[pltpu.VMEM(a.shape, a.dtype) for a in args],
+            pltpu.VMEM(window.shape, F32),
+            pltpu.VMEM(window.shape, F32),
+            pltpu.VMEM(blocks.shape, BF16),
+            dma(6),
+            dma(count),
+            dma(count),
+            dma(count),
+        ],
+        landed=[0],
+        streams=range(6),
+        out_streams=range(len(outs)),
+        work=20 * BLOCK * blocks.size,
+    )
+
+
+def correlate(spectrum, window, inverse):
+    count, _, width = spectrum.shape
+    shape = (count, BLOCK, width)
+    args = [spectrum, window, *inverse]
+
+    def body(*refs):
+        sources, y_hbm, targets = refs[:4], refs[4], refs[5:9]
+        prod, y_ref, t_sem, y_sem = refs[9:]
+        leave = copies(y_ref, y_hbm, y_sem)
+        loads = [pltpu.make_async_copy(sources[n], targets[n], t_sem.at[n]) for n in range(4)]
+        for move in loads:
+            move.start()
+        for move in loads:
+            move.wait()
+        s_ref, w_ref, th, tl = targets
+        block_products(w_ref, s_ref, prod, count, width, True)
+        for b in range(count):
+            y_ref[b] = inverse_block(prod[b], th[...], tl[...]).astype(BF16)
+            leave(b).start()
+        for b in range(count):
+            leave(b).wait()
+
+    return whole(
+        body,
+        "correlate",
+        args,
+        [stored(shape, BF16)],
+        [
+            *[pltpu.VMEM(a.shape, a.dtype) for a in args],
+            pltpu.VMEM(window.shape, F32),
+            pltpu.VMEM(shape, BF16),
+            dma(4),
+            dma(count),
+        ],
+        streams=range(4),
+        out_streams=[0],
+        work=12 * BLOCK * spectrum.size,
+    )[0]
+
+
+def row_sums(features, conv, gain, out_grad):
+    count, tokens, width = conv.shape
+
+    def body(q_hbm, c_hbm, g_ref, o_hbm, s_ref, q_ref, z_ref, o_ref, acc, q_sem, z_sem, o_sem):
+        moves = [
+            copies(c_hbm, z_ref, z_sem),
+            wide_copies(q_hbm.at[0], q_ref, q_sem, width),
+            wide_copies(o_hbm, o_ref, o_sem, width),
+        ]
+
+        def begin(j):
+            for move in moves:
+                move(j).start()
+
+        each(count, begin)
+        acc[...] = jnp.zeros_like(acc)
+
+        def step(j):
+            for move in moves:
+                move(j).wait()
+            for part, cols in parts_of(width):
+                gated = q_ref[j, :, cols].astype(F32) * z_ref[j, :, cols].astype(F32)
+                scaled = o_ref[j, :, cols].astype(F32) * g_ref[:, lane_tile(j, width, part)]
+                acc[0] += gated * gated
+                acc[1] += scaled * gated
+
+        each(count, step)
+        lane = lax.broadcasted_iota(jnp.int32, (tokens, LANES), 1)
+        first = jnp.sum(acc[0], axis=1, keepdims=True)
+        second = jnp.sum(acc[1], axis=1, keepdims=True)
+        s_ref[...] = jnp.where(lane == 0, first, second).T[:8, :]
+
+    return whole(
+        body,
+        "row_sums",
+        [features, conv, gain, out_grad],
+        [kept((8, tokens), F32), *[kept(conv.shape, BF16)] * 3],
+        [pltpu.VMEM((2, tokens, LANES), F32), dma(count), dma(count), dma(count)],
+        landed=[1],
+        streams=[0, 1, 3],
+        work=6 * conv.size,
+    )
+
+
+def row_scales(sums, tokens):
+    turned = jnp.concatenate([sums] * (tokens // 8), axis=0).T
+    rscale = lax.rsqrt(turned[:, 0:1] * (1.0 / D) + epsilon)
+    return rscale, rscale * turned[:, 1:2] * (1.0 / D)
+
+
+def conv_grads(gate, conv, out_grad, gain, own_sums, other_sums):
+    count, tokens, width = conv.shape
+
+    def body(q_ref, z_ref, o_ref, g_ref, s_ref, r_ref, d_hbm, t_hbm, chunks, total, d_sem, t_sem):
+        leave = copies(chunks, d_hbm, d_sem)
+        total[...] = s_ref[...] + r_ref[...]
+        keep = pltpu.make_async_copy(total, t_hbm, t_sem.at[0])
+        keep.start()
+        rscale, inner = row_scales(total[...], tokens)
+        factor = rscale * inner * rscale
+        rscale = jnp.broadcast_to(rscale, (tokens, LANES))
+        factor = jnp.broadcast_to(factor, (tokens, LANES))
+
+        def step(j):
+            for part, cols in parts_of(width):
+                gate_feat = q_ref[j, :, cols].astype(F32)
+                gated = gate_feat * z_ref[j, :, cols].astype(F32)
+                scaled = o_ref[j, :, cols].astype(F32) * g_ref[:, lane_tile(j, width, part)]
+                grad = (rscale * scaled - factor * gated) * gate_feat
+                chunks[j, :, cols] = grad.astype(BF16)
+            leave(j).start()
+
+        each(count, step)
+        keep.wait()
+        each(count, lambda j: leave(j).wait())
+
+    return whole(
+        body,
+        "conv_grads",
+        [*map(held, [gate, conv, out_grad]), gain, held(own_sums), other_sums],
+        [stored(conv.shape, BF16), stored(own_sums.shape, F32)],
+        [pltpu.VMEM(conv.shape, BF16), pltpu.VMEM(own_sums.shape, F32), dma(count), dma(1)],
+        out_streams=[0, 1],
+        work=8 * conv.size,
+    )
+
+
+def norm_outputs(features, conv, gain, out_grad, sums, projections, edges, groups):
+    count, tokens, width = conv.shape
+    local = count * width
+
+    def body(q_hbm, c_hbm, g_ref, o_hbm, s_ref, p_hbm, e_ref, out_hbm, gg_hbm, rows_ref, *scratch):
+        q_ref, z_ref, o_ref, p_ref, out, gg, ext, sums, gains, sems, out_sem, gg_sem = scratch
+        moves = [
+            copies(c_hbm, z_ref, sems.at[0]),
+            wide_copies(q_hbm.at[0], q_ref, sems.at[1], width),
+            wide_copies(o_hbm, o_ref, sems.at[2], width),
+            wide_copies(p_hbm.at[0], p_ref, sems.at[3], width),
+        ]
+        stores = [wide_stores(out, out_hbm, out_sem, width), wide_stores(gg, gg_hbm, gg_sem, width)]
+
+        def begin(j):
+            for move in moves:
+                move(j).start()
+
+        each(count, begin)
+        sums[...] = jnp.zeros_like(sums)
+        rscale, inner = row_scales(s_ref[...], tokens)
+        rscale = jnp.broadcast_to(rscale, (tokens, LANES))
+        inner = jnp.broadcast_to(inner, (tokens, LANES))
+
+        def step(j):
+            for move in moves:
+                move(j).wait()
+            for part, cols in parts_of(width):
+                here = lane_tile(j, width, part)
+                conv_out = z_ref[j, :, cols].astype(F32)
+                grad = o_ref[j, :, cols].astype(F32)
+                gain_row = g_ref[:, here]
+                normed = q_ref[j, :, cols].astype(F32) * conv_out * rscale
+                out[j, :, cols] = (normed * gain_row).astype(BF16)
+                grad_gated = rscale * (grad * gain_row - normed * inner)
+                own = grad_gated * conv_out
+                gg[j, :, cols] = own.astype(BF16)
+                gains[:, here] = jnp.sum(grad * normed, axis=0, keepdims=True)
+                before, values = e_ref[0, :, here], p_ref[j, :, cols]
+                tap_sums(own, before, values, ext, sums, j, 0, cols, tokens)
+            for store in stores:
+                store(j).start()
+
+        def finish(j):
+            for store in stores:
+                store(j).wait()
+
+        each(count, step)
+        for j in range(count):
+            rows_ref[j : j + 1] = gains[:, j * width : (j + 1) * width]
+        gather_groups(sums, rows_ref.at[count:], groups, width)
+        each(count, finish)
+
+    chunk = pltpu.VMEM(conv.shape, BF16)
+    return whole(
+        body,
+        "norm_outputs",
+        [features, conv, gain, out_grad, sums, projections, edges],
+        [
+            stored((tokens, local), BF16),
+            stored((tokens, local), BF16),
+            shape_of((count + KS + 1, groups), F32),
+        ],
+        [
+            *[chunk] * 6,
+            pltpu.VMEM((HALO + tokens, LANES), F32),
+            pltpu.VMEM((count, KS + 1, width), F32),
+            pltpu.VMEM((1, local), F32),
+            dma(4, count),
+            dma(count),
+            dma(count),
+        ],
+        landed=[1],
+        streams=[0, 1, 3, 5],
+        out_streams=[0, 1],
+        work=28 * conv.size,
+    )
+
+
+def shape_of(shape, dtype):
+    return jax.ShapeDtypeStruct(shape, dtype)
+
+
+def tap_sums(own, before, values, ext, sums, j, first, cols, tokens):
+    ext[:HALO, :] = before.astype(F32)
+    ext[HALO:, :] = values.astype(F32)
+    for tap in range(KS):
+        total = jnp.sum(own * ext[HALO - tap : HALO - tap + tokens, :], axis=0, keepdims=True)
+        sums[j, first + tap : first + tap + 1, cols] = total
+
+
+def mix_tap_sums(mix, features, projections, edges, groups):
+    count, tokens, width = mix.shape
+    local = count * width
+
+    def body(m_hbm, f_hbm, p_hbm, e_ref, out_ref, m_ref, f_ref, p_ref, ext, sums, sems):
+        moves = [
+            copies(m_hbm, m_ref, sems.at[0]),
+            wide_copies(f_hbm.at[1:], f_ref, sems.at[1], width),
+            wide_copies(p_hbm.at[1:], p_ref, sems.at[2], width),
+        ]
+
+        def begin(j):
+            for move in moves:
+                move(j).start()
+
+        each(count, begin)
+        sums[...] = jnp.zeros_like(sums)
+
+        def step(j):
+            for move in moves:
+                move(j).wait()
+            for part, cols in parts_of(width):
+                here = lane_tile(j, width, part)
+                mixed = m_ref[j, :, cols].astype(F32)
+                for i in (1, 2):
+                    own = mixed * f_ref[j, 2 - i, :, cols].astype(F32)
+                    before, values = e_ref[i, :, here], p_ref[j, i - 1, :, cols]
+                    tap_sums(own, before, values, ext, sums, j, (i - 1) * KS, cols, tokens)
+
+        each(count, step)
+        gather_groups(sums, out_ref, groups, width)
+
+    return whole(
+        body,
+        "mix_tap_sums",
+        [mix, features, projections, edges],
+        [shape_of((2 * KS + 2, groups), F32)],
+        [
+            pltpu.VMEM(mix.shape, BF16),
+            pltpu.VMEM((count, 2, tokens, width), BF16),
+            pltpu.VMEM((count, 2, tokens, width), BF16),
+            pltpu.VMEM((HALO + tokens, LANES), F32),
+            pltpu.VMEM((count, 2 * KS + 2, width), F32),
+            dma(3, count),
+        ],
+        landed=[0],
+        streams=[0, 1, 2],
+        work=28 * tokens * local,
+    )[0]
+
+
+def proj_grads_of(mix, mix_halo, gate_grad, gate_halo, features, feat_halo, per_chan):
+    count, tokens, width = mix.shape
+    local = count * width
+
+    def body(m_hbm, mh_ref, gg_hbm, gh_ref, f_hbm, fh_ref, t_ref, o_hbm, *scratch):
+        m_ref, gg_ref, f_ref, out, grads, sems, out_sem = scratch
+        moves = [
+            copies(m_hbm, m_ref, sems.at[0]),
+            wide_copies(gg_hbm, gg_ref, sems.at[1], width),
+            wide_copies(f_hbm.at[1:], f_ref, sems.at[2], width),
+        ]
+        leave = wide_stores(out, o_hbm, out_sem, width)
+
+        def begin(j):
+            for move in moves:
+                move(j).start()
+
+        each(count, begin)
+
+        def step(j):
+            for move in moves:
+                move(j).wait()
+            for part, cols in parts_of(width):
+                here = lane_tile(j, width, part)
+                rows = t_ref[:, here]
+                mixed = m_ref[j, :, cols].astype(F32)
+                mixed_after = mh_ref[j, :, cols].astype(F32)
+                for i in range(3):
+                    if i == 0:
+                        own = gg_ref[j, :, cols].astype(F32)
+                        after = gh_ref[:, here].astype(F32)
+                    else:
+                        own = mixed * f_ref[j, 2 - i, :, cols].astype(F32)
+                        after = mixed_after * fh_ref[3 - i, :, here].astype(F32)
+                    grads[i, :tokens, :] = own
+                    grads[i, tokens:, :] = after
+                    total = None
+                    for tap in range(KS):
+                        at = i * KS + tap
+                        term = rows[at : at + 1] * grads[i, tap : tap + tokens, :]
+                        total = term if total is None else total + term
+                    out[j, i, :, cols] = total.astype(BF16)
+            leave(j).start()
+
+        each(count, step)
+        each(count, lambda j: leave(j).wait())
+
+    return whole(
+        body,
+        "proj_grads",
+        [mix, mix_halo, gate_grad, gate_halo, features, feat_halo, per_chan],
+        [stored((3, tokens, local), BF16)],
+        [
+            pltpu.VMEM(mix.shape, BF16),
+            pltpu.VMEM(mix.shape, BF16),
+            pltpu.VMEM((count, 2, tokens, width), BF16),
+            pltpu.VMEM((count, 3, tokens, width), BF16),
+            pltpu.VMEM((3, HALO + tokens, LANES), F32),
+            dma(3, count),
+            dma(count),
+        ],
+        landed=[0],
+        streams=[0, 2, 4],
+        out_streams=[0],
+        work=48 * tokens * local,
+    )[0]
+
+
+def exchange(values, axis, distance):
+    size = lax.axis_size(axis)
+    return lax.ppermute(values, axis, [(i, i ^ distance) for i in range(size)])
+
+
+def butterfly_sum(values, axis):
+    distance = 1
+    while distance < lax.axis_size(axis):
+        values = values + exchange(values, axis, distance)
+        distance *= 2
+    return values
+
+
+def swap_blocks(chunks):
+    return lax.all_to_all(chunks, "ctx", split_axis=0, concat_axis=0, tiled=True)
+
+
+def together(*values):
+    return lax.optimization_barrier(values)
+
+
+def kernel_path(projections, grouped_short_filters, long_filter, norm_gain, out_grad):
+    tokens, local = projections.shape[1:]
+    spread = lax.axis_size("ctx")
+    width = local // spread
+    count = tokens * spread // BLOCK
+    groups = local // GROUP
+
+    def as_blocks(chunks):
+        return chunks.reshape(count, BLOCK, width)
+
+    def as_chunks(blocks):
+        return blocks.reshape(spread, tokens, width)
+
+    taps = jnp.pad(grouped_short_filters.reshape(3 * KS, groups), ((0, 3), (0, 0)))
+    edges = passed_along(projections[:, tokens - HALO :, :], "ctx", 1)
+    sent_h = to_chunks(long_filter, width)
+    edges, sent_h = together(edges, sent_h)
+    chan_h = swap_blocks(sent_h)
+    tables = forward, inverse = jax.tree.map(jnp.asarray, block_tables())
+    gain = norm_gain.reshape(1, local)
+    per_chan = spread_taps(taps, local, width)
+    features, mixed = short_conv(projections, edges, per_chan, width)
+    chan_h, mixed = together(chan_h, mixed)
+    chan_u = swap_blocks(mixed)
+    window_h = window_spectrum(as_blocks(chan_h), forward)
+    feat_halo = passed_along(features[:, :HALO, :], "ctx", -1)
+    chan_u, window_h, feat_halo = together(chan_u, window_h, feat_halo)
+    (chan_z,) = convolve(as_blocks(chan_u), window_h, tables, False)
+    conv = swap_blocks(as_chunks(chan_z))
+    window_u = window_spectrum(as_blocks(chan_u), forward)
+    conv, window_u = together(conv, window_u)
+    own_sums, *near = row_sums(features, conv, gain, out_grad)
+    grad_conv, sums = conv_grads(*near, gain, own_sums, exchange(own_sums, "ch", 1))
+    chan_d = swap_blocks(grad_conv)
+    output, gate_grad, early = norm_outputs(
+        features, conv, gain, out_grad, sums, projections, edges, groups
+    )
+    gate_halo = passed_along(gate_grad[:HALO, :], "ctx", -1)
+    chan_d, output, gate_grad, early = together(chan_d, output, gate_grad, early)
+    chan_du, spec_d = convolve(as_blocks(chan_d), window_h, tables, True)
+    mix = swap_blocks(as_chunks(chan_du))
+    chan_dh = correlate(spec_d, window_u, inverse)
+    chan_dh, early = together(chan_dh, early)
+    early = butterfly_sum(early, "ctx")
+    mix, chan_dh, gate_halo, early = together(mix, chan_dh, gate_halo, early)
+    filt = swap_blocks(as_chunks(chan_dh))
+    mix_halo = passed_along(mix[:, :HALO, :], "ctx", -1)
+    late = mix_tap_sums(mix, features, projections, edges, groups)
+    late = butterfly_sum(late, "ctx")
+    proj_grads = proj_grads_of(mix, mix_halo, gate_grad, gate_halo, features, feat_halo, per_chan)
+    short_grads = jnp.concatenate([early[spread : spread + KS], late[: 2 * KS]], axis=0)
+    return (
+        output,
+        proj_grads,
+        short_grads.reshape(3, KS, groups),
+        from_chunks(filt),
+        early[:spread].reshape(local),
+    )
+
+
+def on_device(projections, grouped_short_filters, long_filter, norm_gain, out_grad):
+    tokens, local = projections.shape[1:]
+    spread = lax.axis_size("ctx")
+    width = local // spread
+    length = tokens * spread
+    whole_tiles = width % LANES == 0 and tokens == LANES and length % BLOCK == 0
+    pairs = spread & (spread - 1) == 0 and lax.axis_size("ch") == 2
+    fits = whole_tiles and pairs and length <= 8 * BLOCK and width == local // GROUP
+    path = kernel_path if fits else narrow_path
+    return path(projections, grouped_short_filters, long_filter, norm_gain, out_grad)
+
+
 def solution(mesh):
     in_specs = (P(None, "ctx", "ch"), P(None, None, "ch"), P("ctx", "ch"), P("ch"), P("ctx", "ch"))
     out_specs = (P("ctx", "ch"), P(None, "ctx", "ch"), P(None, None, "ch"), P("ctx", "ch"), P("ch"))

time: 699 us -> 236 us (0.34)
  matrix products: 245 us -> 0 us
  blocking collectives: 134 us -> 0 us
  other arithmetic: 105 us -> 0.05 us
  Pallas kernels: 0 us -> 78.6 us
  local copies, waits for them, and re-layouts: 66.3 us -> 4.68 us
  starting transfers between devices: 50.2 us -> 68 us
  waiting for transfers between devices: 90.7 us -> 82.3 us
    dot_general x36 -> x0, matrix products: 245 us -> none  [contract(): return jnp.einsum(form, left, right, precision=lax.Precision.HIGHEST)]
    pallas_call x0 -> x14, Pallas kernels: none -> 78.6 us  [whole(): pl.pallas_call(body, name=name, in_specs=[ANY if i in streams else VMEM f...]
    psum x3 -> x0, blocking collectives: 75.5 us -> none  [the longest x1 65.7 us: on_device(): gain_grad, short_grads = lax.psum((gain_part, filt_part), 'ctx')]
    all_to_all x1 -> x0, blocking collectives: 58.2 us -> none  [on_device(): lax.all_to_all(grad_conv.T, 'ctx', split_axis=0, concat_axis=1, tiled=True)]
    convert_element_type x2 -> x0, other arithmetic: 54.3 us -> none  [the longest x1 28.2 us: on_device(): grad_in.astype(jnp.bfloat16)]
    all_to_all x5 -> x6, waiting for transfers between devices: 90.7 us -> 61.8 us  [swap_blocks(): lax.all_to_all(chunks, 'ctx', split_axis=0, concat_axis=0, tiled=True)]
    reduce_sum x10 -> x0, other arithmetic: 28 us -> none  [the longest x1 21.9 us: on_device(): tap_prod = jnp.sum(grad_feats * window, axis=1)]
    unnamed x81 -> x8, local copies, waits for them, and re-layouts: 24.7 us -> 1.31 us
  transfers between devices with their start and end apart: 7 -> 19, of which waited for: 3 -> 13; matrix products, arithmetic and copies ran while one was open for 17% -> 1% of each run, Pallas kernels for 0% -> 21%
where the time goes in v1:
time: 236 us; the launch traced here: 235 us
  waiting for transfers between devices  82.3 us (35%)
  Pallas kernels  78.6 us (33%)
  starting transfers between devices  68 us (29%)
  local copies, waits for them, and re-layouts  4.68 us (2%)
    pallas_call x14, Pallas kernels, whole(): pl.pallas_call(body, name=name, in_specs=[ANY if i in streams else VMEM f...  78.6 us
    all_to_all x6, waiting for transfers between devices, swap_blocks(): lax.all_to_all(chunks, 'ctx', split_axis=0, concat_axis=0, tiled=True)  61.8 us
    all_to_all x6, starting transfers between devices, swap_blocks(): lax.all_to_all(chunks, 'ctx', split_axis=0, concat_axis=0, tiled=True)  41.5 us
    ppermute x9, waiting for transfers between devices, exchange(): return lax.ppermute(values, axis, [(i, i ^ distance) for i in range(size)])  20.4 us
    ppermute x9, starting transfers between devices, exchange(): return lax.ppermute(values, axis, [(i, i ^ distance) for i in range(size)])  20.2 us
    ppermute x4, starting transfers between devices, passed_along(): return lax.ppermute(block, axis, route)  6.26 us
  transfers between devices with their start and end apart: 19, of which 13 were waited for; matrix products, arithmetic and copies ran while one was open for 1% of the time, Pallas kernels for 21%

profile of v1, /device:TPU:0, one launch (start us, length us, event | category | flops | bytes accessed | tf_op | source)
XLA Modules:
  0.0 234.7 jit_solution(6860524121182848826)
XLA Ops:
  0.6 0.9 slice.21
  1.6 2.4 %collective-permute-start = (bf16[3,8,4096]{2,1,0:T(8,128)(2,1)S(1)}, bf16[3,8,4096]{2,1,0:T(8,128)(2,1)S(1)}, u32[]{:S(2)}, u32[]{:S(2)}) collective-permute-start(bf16[3,8,4096]{2,1,0:T(8,128)(2,1)S(1)} %slice.21), channel_id=1, source_target_pairs={{0,2},{2,4},{4,6},{6,8},{8,10},{10,12},{12,14},{14,16},{16,18},{18... | collective-permute-start | bytes 589832 | tf_op jit(solution)/shard_map/ppermute | solution.py:25
  4.0 2.5 %to_chunks.1 = bf16[16,128,256]{2,1,0:T(8,128)(2,1)} custom-call(f32[128,4096]{1,0:T(8,128)} %source.1), custom_call_target="tpu_custom_call" | custom-call | bytes 3145728 | tf_op jit(solution)/shard_map/to_chunks/pallas_call | solution.py:207
  6.6 9.4 %all-to-all-start = ((bf16[16,128,256]{2,1,0:T(8,128)(2,1)}), bf16[16,128,256]{2,1,0:T(8,128)(2,1)S(1)}, u32[]{:S(2)}, u32[]{:S(2)}) async-start(bf16[16,128,256]{2,1,0:T(8,128)(2,1)} %to_chunks.1), calls=%async_computation | async-start | bytes 2097152 | tf_op jit(solution)/shard_map/all_to_all | solution.py:942
  16.0 3.2 %spread_taps.1.t_ref = f32[24,4096]{1,0:T(8,128)S(1)} custom-call(f32[24,256]{1,0:T(8,128)S(1)} %pad.4.t_ref), custom_call_target="tpu_custom_call" | custom-call | flops 100663296 | bytes 417792 | tf_op jit(solution)/shard_map/spread_taps/pallas_call | solution.py:207
  19.2 6.1 %short_conv.1 = (bf16[3,128,4096]{2,1,0:T(8,128)(2,1)}, bf16[16,128,256]{2,1,0:T(8,128)(2,1)}) custom-call(bf16[3,128,4096]{2,1,0:T(8,128)(2,1)} %p_hbm.5, bf16[3,8,4096]{2,1,0:T(8,128)(2,1)S(1)} %collective-permute-done.e_ref, f32[24,4096]{1,0:T(8,128)S(1)} %spread_taps.1.t_ref), custom_call_target="tpu_custom_call" | custom-call | flops 22020096 | bytes 7929856 | tf_op jit(solution)/shard_map/short_conv/pallas_call | solution.py:207
  25.4 13.5 %all-to-all-done = bf16[16,128,256]{2,1,0:T(8,128)(2,1)S(1)} async-done(((bf16[16,128,256]{2,1,0:T(8,128)(2,1)}), bf16[16,128,256]{2,1,0:T(8,128)(2,1)S(1)}, u32[]{:S(2)}, u32[]{:S(2)}) %all-to-all-start) | async-done | bytes 1048608 | tf_op jit(solution)/shard_map/all_to_all | solution.py:942
  38.9 6.8 %all-to-all-start.1 = ((bf16[16,128,256]{2,1,0:T(8,128)(2,1)}), bf16[16,128,256]{2,1,0:T(8,128)(2,1)S(1)}, u32[]{:S(2)}, u32[]{:S(2)}) async-start(bf16[16,128,256]{2,1,0:T(8,128)(2,1)} %get-tuple-element.41), calls=%async_computation.1 | async-start | bytes 2097152 | tf_op jit(solution)/shard_map/all_to_all | solution.py:942
  45.7 0.9 slice.22
  46.6 1.3 collective-permute-start.1
  47.9 5.7 %window_spectrum.2.refs_1_ = f32[8,512,256]{2,1,0:T(8,128)} custom-call(bf16[8,256,256]{2,1,0:T(8,128)(2,1)S(1)} %bitcast.10, bf16[512,256]{1,0:T(8,128)(2,1)} %constant.11.clone.hi_hbm.refs_2_, bf16[512,256]{1,0:T(8,128)(2,1)} %constant.12.clone.lo_hbm.refs_3_), custom_call_target="tpu_custom_call" | custom-call | flops 1073741824 | bytes 5767168 | tf_op jit(solution)/shard_map/window_spectrum/pallas_call | solution.py:207
  53.7 14.9 %all-to-all-done.1 = bf16[16,128,256]{2,1,0:T(8,128)(2,1)S(1)} async-done(((bf16[16,128,256]{2,1,0:T(8,128)(2,1)}), bf16[16,128,256]{2,1,0:T(8,128)(2,1)S(1)}, u32[]{:S(2)}, u32[]{:S(2)}) %all-to-all-start.1) | async-done | bytes 1048608 | tf_op jit(solution)/shard_map/all_to_all | solution.py:942
  68.6 10.1 %convolve.1 = bf16[8,256,256]{2,1,0:T(8,128)(2,1)} custom-call(bf16[8,256,256]{2,1,0:T(8,128)(2,1)S(1)} %bitcast.11, f32[8,512,256]{2,1,0:T(8,128)} %window_spectrum.2.refs_1_, bf16[512,256]{1,0:T(8,128)(2,1)} %constant.11.clone.hi_hbm.refs_2_, bf16[512,256]{1,0:T(8,128)(2,1)} %constant.12.clone.lo_hbm.refs_3_, ...), custom_call_target="tpu_custom_call" | custom-call | flops 2684354560 | bytes 7340032 | tf_op jit(solution)/shard_map/convolve/pallas_call | solution.py:207
  78.7 8.0 %all-to-all-start.2 = ((bf16[16,128,256]{2,1,0:T(8,128)(2,1)}), bf16[16,128,256]{2,1,0:T(8,128)(2,1)S(1)}, u32[]{:S(2)}, u32[]{:S(2)}) async-start(bf16[16,128,256]{2,1,0:T(8,128)(2,1)} %bitcast.19), calls=%async_computation.2 | async-start | bytes 2097152 | tf_op jit(solution)/shard_map/all_to_all | solution.py:942
  86.8 5.7 %window_spectrum.3.refs_1_ = f32[8,512,256]{2,1,0:T(8,128)} custom-call(bf16[8,256,256]{2,1,0:T(8,128)(2,1)S(1)} %bitcast.12, bf16[512,256]{1,0:T(8,128)(2,1)} %constant.11.clone.hi_hbm.refs_2_, bf16[512,256]{1,0:T(8,128)(2,1)} %constant.12.clone.lo_hbm.refs_3_), custom_call_target="tpu_custom_call" | custom-call | flops 1073741824 | bytes 5767168 | tf_op jit(solution)/shard_map/window_spectrum/pallas_call | solution.py:207
  92.5 17.2 %all-to-all-done.2.c_hbm = bf16[16,128,256]{2,1,0:T(8,128)(2,1)S(1)} async-done(((bf16[16,128,256]{2,1,0:T(8,128)(2,1)}), bf16[16,128,256]{2,1,0:T(8,128)(2,1)S(1)}, u32[]{:S(2)}, u32[]{:S(2)}) %all-to-all-start.2) | async-done | bytes 1048608 | tf_op jit(solution)/shard_map/all_to_all | solution.py:942
  109.6 3.1 %row_sums.1 = (f32[8,128]{1,0:T(8,128)S(1)}, bf16[16,128,256]{2,1,0:T(8,128)(2,1)S(1)}, bf16[16,128,256]{2,1,0:T(8,128)(2,1)S(1)}, bf16[16,128,256]{2,1,0:T(8,128)(2,1)S(1)}) custom-call(bf16[3,128,4096]{2,1,0:T(8,128)(2,1)} %get-tuple-element.38.q_hbm.f_hbm, bf16[16,128,256]{2,1,0:T(8,128)(2,1)S(1)} %all-to-all-done.2.c_hbm, f32[1,4096]{1,0:T(1,128)S(1)} %bitcast.14, ...), custom_call_target="tpu_custom_call" | custom-call | flops 3145728 | bytes 8409088 | tf_op jit(solution)/shard_map/row_sums/pallas_call | solution.py:207
  112.7 1.6 collective-permute-start.2
  114.3 2.1 collective-permute-done.2.r_ref
  116.4 1.8 conv_grads.1
  118.2 6.8 %all-to-all-start.3 = ((bf16[16,128,256]{2,1,0:T(8,128)(2,1)}), bf16[16,128,256]{2,1,0:T(8,128)(2,1)S(1)}, u32[]{:S(2)}, u32[]{:S(2)}) async-start(bf16[16,128,256]{2,1,0:T(8,128)(2,1)} %get-tuple-element.50), calls=%async_computation.3 | async-start | bytes 2097152 | tf_op jit(solution)/shard_map/all_to_all | solution.py:942
  125.0 0.7 copy-done.1
  125.7 6.0 %norm_outputs.1 = (bf16[128,4096]{1,0:T(8,128)(2,1)}, bf16[128,4096]{1,0:T(8,128)(2,1)}, f32[24,256]{1,0:T(8,128)S(1)}) custom-call(bf16[3,128,4096]{2,1,0:T(8,128)(2,1)} %get-tuple-element.38.q_hbm.f_hbm, bf16[16,128,256]{2,1,0:T(8,128)(2,1)S(1)} %all-to-all-done.2.c_hbm, f32[1,4096]{1,0:T(1,128)S(1)} %bitcast.16, bf16[128,4096]{1,0:T(8,128)(2,1)} %o_hbm.3, ...), custom_call_target="tpu_custom_call" | custom-call | flops 14680064 | bytes 10727424 | tf_op jit(solution)/shard_map/norm_outputs/pallas_call | solution.py:207
  131.7 16.2 %all-to-all-done.3 = bf16[16,128,256]{2,1,0:T(8,128)(2,1)S(1)} async-done(((bf16[16,128,256]{2,1,0:T(8,128)(2,1)}), bf16[16,128,256]{2,1,0:T(8,128)(2,1)S(1)}, u32[]{:S(2)}, u32[]{:S(2)}) %all-to-all-start.3) | async-done | bytes 1048608 | tf_op jit(solution)/shard_map/all_to_all | solution.py:942
  147.9 10.3 %correlate_blocks.1 = (bf16[8,256,256]{2,1,0:T(8,128)(2,1)}, f32[8,512,256]{2,1,0:T(8,128)}) custom-call(bf16[8,256,256]{2,1,0:T(8,128)(2,1)S(1)} %bitcast.13, f32[8,512,256]{2,1,0:T(8,128)} %window_spectrum.2.refs_1_, bf16[512,256]{1,0:T(8,128)(2,1)} %constant.11.clone.hi_hbm.refs_2_, bf16[512,256]{1,0:T(8,128)(2,1)} %constant.12.clone.lo_hbm.refs_3_, ...), custom_call_target="tpu_custom_call" | custom-call | flops 2684354560 | bytes 11534336 | tf_op jit(solution)/shard_map/correlate_blocks/pallas_call | solution.py:207
  158.2 6.8 %all-to-all-start.4 = ((bf16[16,128,256]{2,1,0:T(8,128)(2,1)}), bf16[16,128,256]{2,1,0:T(8,128)(2,1)S(1)}, u32[]{:S(2)}, u32[]{:S(2)}) async-start(bf16[16,128,256]{2,1,0:T(8,128)(2,1)} %bitcast.18), calls=%async_computation.4 | async-start | bytes 2097152 | tf_op jit(solution)/shard_map/all_to_all | solution.py:942
  165.0 8.9 %correlate.1 = bf16[8,256,256]{2,1,0:T(8,128)(2,1)} custom-call(f32[8,512,256]{2,1,0:T(8,128)} %get-tuple-element.58.refs_0_, f32[8,512,256]{2,1,0:T(8,128)} %window_spectrum.3.refs_1_, bf16[256,512]{1,0:T(8,128)(2,1)} %constant.13.clone.refs_4_.refs_2_, bf16[256,512]{1,0:T(8,128)(2,1)} %constant.14.clone.refs_5_.refs_3_), custom_call_target="tpu_custom_call" | custom-call | flops 3221225472 | bytes 9961472 | tf_op jit(solution)/shard_map/correlate/pallas_call | solution.py:207
  174.4 0.8 collective-permute-done.4
  175.3 1.9 collective-permute-start.5
  177.2 0.8 slice.23
  178.0 1.3 collective-permute-start.3
  179.7 1.8 collective-permute-start.6
  181.5 2.7 %collective-permute-done.6 = f32[24,256]{1,0:T(8,128)S(1)} collective-permute-done((f32[24,256]{1,0:T(8,128)S(1)}, f32[24,256]{1,0:T(8,128)S(1)}, u32[]{:S(2)}, u32[]{:S(2)}) %collective-permute-start.6) | collective-permute-done | bytes 24608 | tf_op jit(solution)/shard_map/ppermute | solution.py:930
  184.1 4.6 %collective-permute-start.7 = (f32[24,256]{1,0:T(8,128)S(1)}, f32[24,256]{1,0:T(8,128)S(1)}, u32[]{:S(2)}, u32[]{:S(2)}) collective-permute-start(f32[24,256]{1,0:T(8,128)S(1)} %add.28), channel_id=1, source_target_pairs={{0,16},{2,18},{4,20},{6,22},{8,24},{10,26},{12,28},{14,30},{16,0},... | collective-permute-start | bytes 73736 | tf_op jit(solution)/shard_map/ppermute | solution.py:930
  188.7 4.6 %collective-permute-done.7 = f32[24,256]{1,0:T(8,128)S(1)} collective-permute-done((f32[24,256]{1,0:T(8,128)S(1)}, f32[24,256]{1,0:T(8,128)S(1)}, u32[]{:S(2)}, u32[]{:S(2)}) %collective-permute-start.7) | collective-permute-done | bytes 24608 | tf_op jit(solution)/shard_map/ppermute | solution.py:930
  193.3 3.7 %all-to-all-start.5 = ((bf16[16,128,256]{2,1,0:T(8,128)(2,1)}), bf16[16,128,256]{2,1,0:T(8,128)(2,1)S(1)}, u32[]{:S(2)}, u32[]{:S(2)}) async-start(bf16[16,128,256]{2,1,0:T(8,128)(2,1)} %bitcast.17), calls=%async_computation.5 | async-start | bytes 2097152 | tf_op jit(solution)/shard_map/all_to_all | solution.py:942
  197.0 5.4 %mix_tap_sums.1 = f32[16,256]{1,0:T(8,128)S(1)} custom-call(bf16[16,128,256]{2,1,0:T(8,128)(2,1)S(1)} %all-to-all-done.4.m_hbm, bf16[3,128,4096]{2,1,0:T(8,128)(2,1)} %get-tuple-element.38.q_hbm.f_hbm, bf16[3,128,4096]{2,1,0:T(8,128)(2,1)} %p_hbm.5, bf16[3,8,4096]{2,1,0:T(8,128)(2,1)S(1)} %collective-permute-done.e_ref), custom_call_target="tpu_custom_call" | custom-call | flops 14680064 | bytes 7553024 | tf_op jit(solution)/shard_map/mix_tap_sums/pallas_call | solution.py:207
  202.8 0.9 collective-permute-done.9
  203.7 1.8 collective-permute-start.10
  205.5 2.2 collective-permute-done.10
  207.6 3.2 %collective-permute-start.11 = (f32[16,256]{1,0:T(8,128)S(1)}, f32[16,256]{1,0:T(8,128)S(1)}, u32[]{:S(2)}, u32[]{:S(2)}) collective-permute-start(f32[16,256]{1,0:T(8,128)S(1)} %add.31), channel_id=1, source_target_pairs={{0,8},{2,10},{4,12},{6,14},{8,0},{10,2},{12,4},{14,6},{16,24},{18,... | collective-permute-start | bytes 49160 | tf_op jit(solution)/shard_map/ppermute | solution.py:930
  210.9 4.3 %collective-permute-done.11 = f32[16,256]{1,0:T(8,128)S(1)} collective-permute-done((f32[16,256]{1,0:T(8,128)S(1)}, f32[16,256]{1,0:T(8,128)S(1)}, u32[]{:S(2)}, u32[]{:S(2)}) %collective-permute-start.11) | collective-permute-done | bytes 16416 | tf_op jit(solution)/shard_map/ppermute | solution.py:930
  215.2 4.5 %collective-permute-start.12 = (f32[16,256]{1,0:T(8,128)S(1)}, f32[16,256]{1,0:T(8,128)S(1)}, u32[]{:S(2)}, u32[]{:S(2)}) collective-permute-start(f32[16,256]{1,0:T(8,128)S(1)} %add.32), channel_id=1, source_target_pairs={{0,16},{2,18},{4,20},{6,22},{8,24},{10,26},{12,28},{14,30},{16,0},... | collective-permute-start | bytes 49160 | tf_op jit(solution)/shard_map/ppermute | solution.py:930
  219.8 0.6 copy.14
  220.4 1.3 collective-permute-start.8
  221.7 2.5 %collective-permute-done.12 = f32[16,256]{1,0:T(8,128)S(1)} collective-permute-done((f32[16,256]{1,0:T(8,128)S(1)}, f32[16,256]{1,0:T(8,128)S(1)}, u32[]{:S(2)}, u32[]{:S(2)}) %collective-permute-start.12) | collective-permute-done | bytes 16416 | tf_op jit(solution)/shard_map/ppermute | solution.py:930
  224.8 6.8 %proj_grads.1 = bf16[3,128,4096]{2,1,0:T(8,128)(2,1)} custom-call(bf16[16,128,256]{2,1,0:T(8,128)(2,1)S(1)} %all-to-all-done.4.m_hbm, bf16[16,8,256]{2,1,0:T(8,128)(2,1)S(1)} %collective-permute-done.8.mh_ref, bf16[128,4096]{1,0:T(8,128)(2,1)} %get-tuple-element.64.gg_hbm, bf16[8,4096]{1,0:T(8,128)(2,1)S(1)} %collective-permute-done.3.gh_ref, ...), custom_call_target="tpu_custom_call" | custom-call | flops 25165824 | bytes 9109504 | tf_op jit(solution)/shard_map/proj_grads/pallas_call | solution.py:207
  231.6 2.9 %from_chunks.1 = f32[128,4096]{1,0:T(8,128)} custom-call(bf16[16,128,256]{2,1,0:T(8,128)(2,1)S(1)} %all-to-all-done.5.source), custom_call_target="tpu_custom_call" | custom-call | bytes 3145728 | tf_op jit(solution)/shard_map/from_chunks/pallas_call | solution.py:207
  (29 shorter events, 1.9 us)
Async XLA Ops:
  0.6 15.4 %copy-start.2 = (f32[3,7,256]{2,1,0:T(8,128)S(1)}, f32[3,7,256]{2,1,0:T(8,128)}, u32[]{:S(2)}) copy-start(f32[3,7,256]{2,1,0:T(8,128)} %param.10) | copy-start | bytes 64516
  1.6 5.0 %collective-permute-start = (bf16[3,8,4096]{2,1,0:T(8,128)(2,1)S(1)}, bf16[3,8,4096]{2,1,0:T(8,128)(2,1)S(1)}, u32[]{:S(2)}, u32[]{:S(2)}) collective-permute-start(bf16[3,8,4096]{2,1,0:T(8,128)(2,1)S(1)} %slice.21), channel_id=1, source_target_pairs={{0,2},{2,4},{4,6},{6,8},{8,10},{10,12},{12,14},{14,16},{16,18},{18... | collective-permute-start | bytes 589832 | tf_op jit(solution)/shard_map/ppermute | solution.py:25
  6.6 32.3 %all-to-all-start = ((bf16[16,128,256]{2,1,0:T(8,128)(2,1)}), bf16[16,128,256]{2,1,0:T(8,128)(2,1)S(1)}, u32[]{:S(2)}, u32[]{:S(2)}) async-start(bf16[16,128,256]{2,1,0:T(8,128)(2,1)} %to_chunks.1), calls=%async_computation | async-start | bytes 2097152 | tf_op jit(solution)/shard_map/all_to_all | solution.py:942
  38.9 29.7 %all-to-all-start.1 = ((bf16[16,128,256]{2,1,0:T(8,128)(2,1)}), bf16[16,128,256]{2,1,0:T(8,128)(2,1)S(1)}, u32[]{:S(2)}, u32[]{:S(2)}) async-start(bf16[16,128,256]{2,1,0:T(8,128)(2,1)} %get-tuple-element.41), calls=%async_computation.1 | async-start | bytes 2097152 | tf_op jit(solution)/shard_map/all_to_all | solution.py:942
  46.6 7.1 %collective-permute-start.1 = (bf16[3,8,4096]{2,1,0:T(8,128)(2,1)S(1)}, bf16[3,8,4096]{2,1,0:T(8,128)(2,1)S(1)}, u32[]{:S(2)}, u32[]{:S(2)}) collective-permute-start(bf16[3,8,4096]{2,1,0:T(8,128)(2,1)S(1)} %slice.22), channel_id=1, source_target_pairs={{2,0},{4,2},{6,4},{8,6},{10,8},{12,10},{14,12},{16,14},{18,16},{20... | collective-permute-start | bytes 589832 | tf_op jit(solution)/shard_map/ppermute | solution.py:25
  78.7 30.9 %all-to-all-start.2 = ((bf16[16,128,256]{2,1,0:T(8,128)(2,1)}), bf16[16,128,256]{2,1,0:T(8,128)(2,1)S(1)}, u32[]{:S(2)}, u32[]{:S(2)}) async-start(bf16[16,128,256]{2,1,0:T(8,128)(2,1)} %bitcast.19), calls=%async_computation.2 | async-start | bytes 2097152 | tf_op jit(solution)/shard_map/all_to_all | solution.py:942
  86.8 22.9 %copy-start = (f32[4096]{0:T(1024)S(1)}, f32[4096]{0:T(1024)}, u32[]{:S(2)}) copy-start(f32[4096]{0:T(1024)} %param.12) | copy-start | bytes 49156
  112.7 3.7 %collective-permute-start.2 = (f32[8,128]{1,0:T(8,128)S(1)}, f32[8,128]{1,0:T(8,128)S(1)}, u32[]{:S(2)}, u32[]{:S(2)}) collective-permute-start(f32[8,128]{1,0:T(8,128)S(1)} %get-tuple-element.49.s_ref), channel_id=1, source_target_pairs={{0,1},{1,0},{2,3},{3,2},{4,5},{5,4},{6,7},{7,6},{8,9},{9,8},{10,11... | collective-permute-start | bytes 12296 | tf_op jit(solution)/shard_map/ppermute | solution.py:930
  118.2 29.7 %all-to-all-start.3 = ((bf16[16,128,256]{2,1,0:T(8,128)(2,1)}), bf16[16,128,256]{2,1,0:T(8,128)(2,1)S(1)}, u32[]{:S(2)}, u32[]{:S(2)}) async-start(bf16[16,128,256]{2,1,0:T(8,128)(2,1)} %get-tuple-element.50), calls=%async_computation.3 | async-start | bytes 2097152 | tf_op jit(solution)/shard_map/all_to_all | solution.py:942
  125.0 0.7 copy-start.1
  158.2 35.1 %all-to-all-start.4 = ((bf16[16,128,256]{2,1,0:T(8,128)(2,1)}), bf16[16,128,256]{2,1,0:T(8,128)(2,1)S(1)}, u32[]{:S(2)}, u32[]{:S(2)}) async-start(bf16[16,128,256]{2,1,0:T(8,128)(2,1)} %bitcast.18), calls=%async_computation.4 | async-start | bytes 2097152 | tf_op jit(solution)/shard_map/all_to_all | solution.py:942
  174.0 1.3 collective-permute-start.4
  175.3 4.4 %collective-permute-start.5 = (f32[24,256]{1,0:T(8,128)S(1)}, f32[24,256]{1,0:T(8,128)S(1)}, u32[]{:S(2)}, u32[]{:S(2)}) collective-permute-start(f32[24,256]{1,0:T(8,128)S(1)} %add.26), channel_id=1, source_target_pairs={{0,4},{2,6},{4,0},{6,2},{8,12},{10,14},{12,8},{14,10},{16,20},{18,... | collective-permute-start | bytes 73736 | tf_op jit(solution)/shard_map/ppermute | solution.py:930
  178.0 15.3 %collective-permute-start.3 = (bf16[8,4096]{1,0:T(8,128)(2,1)S(1)}, bf16[8,4096]{1,0:T(8,128)(2,1)S(1)}, u32[]{:S(2)}, u32[]{:S(2)}) collective-permute-start(bf16[8,4096]{1,0:T(8,128)(2,1)S(1)} %slice.23), channel_id=1, source_target_pairs={{2,0},{4,2},{6,4},{8,6},{10,8},{12,10},{14,12},{16,14},{18,16},{20... | collective-permute-start | bytes 196616 | tf_op jit(solution)/shard_map/ppermute | solution.py:25
  179.7 4.5 %collective-permute-start.6 = (f32[24,256]{1,0:T(8,128)S(1)}, f32[24,256]{1,0:T(8,128)S(1)}, u32[]{:S(2)}, u32[]{:S(2)}) collective-permute-start(f32[24,256]{1,0:T(8,128)S(1)} %add.27), channel_id=1, source_target_pairs={{0,8},{2,10},{4,12},{6,14},{8,0},{10,2},{12,4},{14,6},{16,24},{18,... | collective-permute-start | bytes 73736 | tf_op jit(solution)/shard_map/ppermute | solution.py:930
  184.1 9.2 %collective-permute-start.7 = (f32[24,256]{1,0:T(8,128)S(1)}, f32[24,256]{1,0:T(8,128)S(1)}, u32[]{:S(2)}, u32[]{:S(2)}) collective-permute-start(f32[24,256]{1,0:T(8,128)S(1)} %add.28), channel_id=1, source_target_pairs={{0,16},{2,18},{4,20},{6,22},{8,24},{10,26},{12,28},{14,30},{16,0},... | collective-permute-start | bytes 73736 | tf_op jit(solution)/shard_map/ppermute | solution.py:930
  193.3 38.2 %all-to-all-start.5 = ((bf16[16,128,256]{2,1,0:T(8,128)(2,1)}), bf16[16,128,256]{2,1,0:T(8,128)(2,1)S(1)}, u32[]{:S(2)}, u32[]{:S(2)}) async-start(bf16[16,128,256]{2,1,0:T(8,128)(2,1)} %bitcast.17), calls=%async_computation.5 | async-start | bytes 2097152 | tf_op jit(solution)/shard_map/all_to_all | solution.py:942
  202.4 1.2 collective-permute-start.9
  203.7 4.0 %collective-permute-start.10 = (f32[16,256]{1,0:T(8,128)S(1)}, f32[16,256]{1,0:T(8,128)S(1)}, u32[]{:S(2)}, u32[]{:S(2)}) collective-permute-start(f32[16,256]{1,0:T(8,128)S(1)} %add.30), channel_id=1, source_target_pairs={{0,4},{2,6},{4,0},{6,2},{8,12},{10,14},{12,8},{14,10},{16,20},{18,... | collective-permute-start | bytes 49160 | tf_op jit(solution)/shard_map/ppermute | solution.py:930
  207.6 7.6 %collective-permute-start.11 = (f32[16,256]{1,0:T(8,128)S(1)}, f32[16,256]{1,0:T(8,128)S(1)}, u32[]{:S(2)}, u32[]{:S(2)}) collective-permute-start(f32[16,256]{1,0:T(8,128)S(1)} %add.31), channel_id=1, source_target_pairs={{0,8},{2,10},{4,12},{6,14},{8,0},{10,2},{12,4},{14,6},{16,24},{18,... | collective-permute-start | bytes 49160 | tf_op jit(solution)/shard_map/ppermute | solution.py:930
  215.2 8.9 %collective-permute-start.12 = (f32[16,256]{1,0:T(8,128)S(1)}, f32[16,256]{1,0:T(8,128)S(1)}, u32[]{:S(2)}, u32[]{:S(2)}) collective-permute-start(f32[16,256]{1,0:T(8,128)S(1)} %add.32), channel_id=1, source_target_pairs={{0,16},{2,18},{4,20},{6,22},{8,24},{10,26},{12,28},{14,30},{16,0},... | collective-permute-start | bytes 49160 | tf_op jit(solution)/shard_map/ppermute | solution.py:930
  220.4 4.4 %collective-permute-start.8 = (bf16[16,8,256]{2,1,0:T(8,128)(2,1)S(1)}, bf16[16,8,256]{2,1,0:T(8,128)(2,1)S(1)}, u32[]{:S(2)}, u32[]{:S(2)}) collective-permute-start(bf16[16,8,256]{2,1,0:T(8,128)(2,1)S(1)} %slice.24), channel_id=1, source_target_pairs={{2,0},{4,2},{6,4},{8,6},{10,8},{12,10},{14,12},{16,14},{18,16},{20... | collective-permute-start | bytes 196616 | tf_op jit(solution)/shard_map/ppermute | solution.py:25

commit v2 on v1

--- a/solution.py
+++ b/solution.py
@@ -1,4 +1,3 @@
-import functools
 import math
 
 import jax
@@ -8,6 +7,7 @@
 from jax.experimental import pallas as pl
 from jax.experimental.pallas import tpu as pltpu
 from jax.sharding import PartitionSpec as P
+
 
 D = 8192
 GROUP = 16
@@ -202,11 +202,10 @@
     return pltpu.with_memory_space_constraint(values, pltpu.HBM)
 
 
-def whole(body, name, args, outs, scratch=(), limit=24, work=0, streams=(), out_streams=(), landed=()):
+def whole(body, args, outs, scratch=(), limit=24, work=0, streams=(), out_streams=(), landed=()):
     size = sum(math.prod(a.shape) * a.dtype.itemsize for a in [*args, *outs])
     return pl.pallas_call(
         body,
-        name=name,
         in_specs=[ANY if i in streams else VMEM for i in range(len(args))],
         out_specs=[ANY if i in out_streams else VMEM for i in range(len(outs))],
         out_shape=list(outs),
@@ -282,7 +281,6 @@
 
     return whole(
         body,
-        "to_chunks",
         [values],
         [stored((count, tokens, width), BF16)],
         [
@@ -315,7 +313,6 @@
 
     return whole(
         body,
-        "from_chunks",
         [chunks],
         [stored((tokens, count * width), F32)],
         [
@@ -356,7 +353,7 @@
         each(local // width, step)
 
     work = 4 * rows * groups * local
-    return whole(body, "spread_taps", [taps], [shape_of((rows, local), F32)], work=work)[0]
+    return whole(body, [taps], [shape_of((rows, local), F32)], work=work)[0]
 
 
 def gather_groups(sums, out_ref, groups, width):
@@ -419,7 +416,6 @@
 
     return whole(
         body,
-        "short_conv",
         [projections, edges, per_chan],
         [stored(projections.shape, BF16), stored((count, tokens, width), BF16)],
         [
@@ -472,7 +468,6 @@
     shape = (count, 2 * BLOCK, width)
     return whole(
         body,
-        "window_spectrum",
         [blocks, *forward],
         [stored(shape, F32)],
         [
@@ -525,7 +520,7 @@
     return mxu(hi, top) + (mxu(lo, top) + mxu(hi, rest))
 
 
-def convolve(blocks, window, tables, adjoint):
+def convolve(blocks, window, tables, spread, adjoint):
     count, _, width = blocks.shape
     args = [blocks, window, *sum(tables, ())]
 
@@ -533,7 +528,15 @@
         sources, refs = refs[:6], refs[6:]
         y_hbm, s_hbm, refs = (refs[0], refs[1], refs[2:]) if adjoint else (refs[0], None, refs[1:])
         x_ref, w_ref, fh, fl, th, tl, spec, prod, y_ref, t_sem, x_sem, y_sem, s_sem = refs
-        arrive, leave = copies(sources[0], x_ref, x_sem), copies(y_ref, y_hbm, y_sem)
+        arrive = copies(sources[0], x_ref, x_sem)
+        shared, chunk, _ = y_hbm.shape
+        tokens = count * BLOCK // shared
+
+        def leave(i):
+            rows = y_ref.at[i * tokens : i * tokens + chunk]
+            return pltpu.make_async_copy(rows, y_hbm.at[i], y_sem.at[i])
+
+        sent = 0
         loads = [
             pltpu.make_async_copy(sources[n], target, t_sem.at[n])
             for n, target in [(2, fh), (3, fl), (1, w_ref), (4, th), (5, tl)]
@@ -555,30 +558,37 @@
         for move in loads[2:]:
             move.wait()
         block_products(w_ref, spec, prod, count, width, adjoint)
+        y_ref[count * BLOCK :, :] = jnp.zeros((y_ref.shape[0] - count * BLOCK, width), BF16)
         for b in range(count):
-            y_ref[b] = inverse_block(prod[b], th[...], tl[...]).astype(BF16)
-            leave(b).start()
-        for b in range(count):
-            leave(b).wait()
-            if adjoint:
+            found = inverse_block(prod[b], th[...], tl[...])
+            y_ref[b * BLOCK : (b + 1) * BLOCK, :] = found.astype(BF16)
+            ready = y_ref.shape[0] if b == count - 1 else (b + 1) * BLOCK
+            while sent < shared and sent * tokens + chunk <= ready:
+                leave(sent).start()
+                sent += 1
+        for i in range(shared):
+            leave(i).wait()
+        if adjoint:
+            for b in range(count):
                 copies(spec, s_hbm, s_sem)(b).wait()
 
-    outs = [stored(blocks.shape, BF16)]
+    extra = HALO if adjoint else 0
+    tokens = count * BLOCK // spread
+    outs = [stored((spread, tokens + extra, width), BF16)]
     if adjoint:
         outs.append(stored(window.shape, F32))
     return whole(
         body,
-        "correlate_blocks" if adjoint else "convolve",
         args,
         outs,
         [
             *[pltpu.VMEM(a.shape, a.dtype) for a in args],
             pltpu.VMEM(window.shape, F32),
             pltpu.VMEM(window.shape, F32),
-            pltpu.VMEM(blocks.shape, BF16),
+            pltpu.VMEM((count * BLOCK + 2 * HALO, width), BF16),
             dma(6),
             dma(count),
-            dma(count),
+            dma(spread),
             dma(count),
         ],
         landed=[0],
@@ -612,7 +622,6 @@
 
     return whole(
         body,
-        "correlate",
         args,
         [stored(shape, BF16)],
         [
@@ -662,7 +671,6 @@
 
     return whole(
         body,
-        "row_sums",
         [features, conv, gain, out_grad],
         [kept((8, tokens), F32), *[kept(conv.shape, BF16)] * 3],
         [pltpu.VMEM((2, tokens, LANES), F32), dma(count), dma(count), dma(count)],
@@ -706,7 +714,6 @@
 
     return whole(
         body,
-        "conv_grads",
         [*map(held, [gate, conv, out_grad]), gain, held(own_sums), other_sums],
         [stored(conv.shape, BF16), stored(own_sums.shape, F32)],
         [pltpu.VMEM(conv.shape, BF16), pltpu.VMEM(own_sums.shape, F32), dma(count), dma(1)],
@@ -771,7 +778,6 @@
     chunk = pltpu.VMEM(conv.shape, BF16)
     return whole(
         body,
-        "norm_outputs",
         [features, conv, gain, out_grad, sums, projections, edges],
         [
             stored((tokens, local), BF16),
@@ -807,8 +813,8 @@
 
 
 def mix_tap_sums(mix, features, projections, edges, groups):
-    count, tokens, width = mix.shape
-    local = count * width
+    count, _, width = mix.shape
+    tokens, local = features.shape[1:]
 
     def body(m_hbm, f_hbm, p_hbm, e_ref, out_ref, m_ref, f_ref, p_ref, ext, sums, sems):
         moves = [
@@ -829,7 +835,7 @@
                 move(j).wait()
             for part, cols in parts_of(width):
                 here = lane_tile(j, width, part)
-                mixed = m_ref[j, :, cols].astype(F32)
+                mixed = m_ref[j, :tokens, cols].astype(F32)
                 for i in (1, 2):
                     own = mixed * f_ref[j, 2 - i, :, cols].astype(F32)
                     before, values = e_ref[i, :, here], p_ref[j, i - 1, :, cols]
@@ -840,7 +846,6 @@
 
     return whole(
         body,
-        "mix_tap_sums",
         [mix, features, projections, edges],
         [shape_of((2 * KS + 2, groups), F32)],
         [
@@ -857,11 +862,11 @@
     )[0]
 
 
-def proj_grads_of(mix, mix_halo, gate_grad, gate_halo, features, feat_halo, per_chan):
-    count, tokens, width = mix.shape
-    local = count * width
-
-    def body(m_hbm, mh_ref, gg_hbm, gh_ref, f_hbm, fh_ref, t_ref, o_hbm, *scratch):
+def proj_grads_of(mix, gate_grad, gate_halo, features, feat_halo, per_chan):
+    count, _, width = mix.shape
+    tokens, local = gate_grad.shape
+
+    def body(m_hbm, gg_hbm, gh_ref, f_hbm, fh_ref, t_ref, o_hbm, *scratch):
         m_ref, gg_ref, f_ref, out, grads, sems, out_sem = scratch
         moves = [
             copies(m_hbm, m_ref, sems.at[0]),
@@ -882,8 +887,8 @@
             for part, cols in parts_of(width):
                 here = lane_tile(j, width, part)
                 rows = t_ref[:, here]
-                mixed = m_ref[j, :, cols].astype(F32)
-                mixed_after = mh_ref[j, :, cols].astype(F32)
+                mixed = m_ref[j, :tokens, cols].astype(F32)
+                mixed_after = m_ref[j, tokens:, cols].astype(F32)
                 for i in range(3):
                     if i == 0:
                         own = gg_ref[j, :, cols].astype(F32)
@@ -906,12 +911,11 @@
 
     return whole(
         body,
-        "proj_grads",
-        [mix, mix_halo, gate_grad, gate_halo, features, feat_halo, per_chan],
+        [mix, gate_grad, gate_halo, features, feat_halo, per_chan],
         [stored((3, tokens, local), BF16)],
         [
             pltpu.VMEM(mix.shape, BF16),
-            pltpu.VMEM(mix.shape, BF16),
+            pltpu.VMEM((count, tokens, width), BF16),
             pltpu.VMEM((count, 2, tokens, width), BF16),
             pltpu.VMEM((count, 3, tokens, width), BF16),
             pltpu.VMEM((3, HALO + tokens, LANES), F32),
@@ -919,7 +923,7 @@
             dma(count),
         ],
         landed=[0],
-        streams=[0, 2, 4],
+        streams=[0, 1, 3],
         out_streams=[0],
         work=48 * tokens * local,
     )[0]
@@ -930,12 +934,10 @@
     return lax.ppermute(values, axis, [(i, i ^ distance) for i in range(size)])
 
 
-def butterfly_sum(values, axis):
-    distance = 1
-    while distance < lax.axis_size(axis):
-        values = values + exchange(values, axis, distance)
-        distance *= 2
-    return values
+def group_sum(values, axis, distances):
+    first, second = distances
+    others = [exchange(values, axis, d) for d in (first, second, first + second)]
+    return (values + others[0]) + (others[1] + others[2])
 
 
 def swap_blocks(chunks):
@@ -973,8 +975,8 @@
     window_h = window_spectrum(as_blocks(chan_h), forward)
     feat_halo = passed_along(features[:, :HALO, :], "ctx", -1)
     chan_u, window_h, feat_halo = together(chan_u, window_h, feat_halo)
-    (chan_z,) = convolve(as_blocks(chan_u), window_h, tables, False)
-    conv = swap_blocks(as_chunks(chan_z))
+    (chan_z,) = convolve(as_blocks(chan_u), window_h, tables, spread, False)
+    conv = swap_blocks(chan_z)
     window_u = window_spectrum(as_blocks(chan_u), forward)
     conv, window_u = together(conv, window_u)
     own_sums, *near = row_sums(features, conv, gain, out_grad)
@@ -984,26 +986,22 @@
         features, conv, gain, out_grad, sums, projections, edges, groups
     )
     gate_halo = passed_along(gate_grad[:HALO, :], "ctx", -1)
+    early = group_sum(early, "ctx", (1, 2))
+    early = early + exchange(early, "ctx", 4)
     chan_d, output, gate_grad, early = together(chan_d, output, gate_grad, early)
-    chan_du, spec_d = convolve(as_blocks(chan_d), window_h, tables, True)
-    mix = swap_blocks(as_chunks(chan_du))
+    chan_du, spec_d = convolve(as_blocks(chan_d), window_h, tables, spread, True)
+    mix = swap_blocks(chan_du)
+    early = early + exchange(early, "ctx", 8)
     chan_dh = correlate(spec_d, window_u, inverse)
-    chan_dh, early = together(chan_dh, early)
-    early = butterfly_sum(early, "ctx")
-    mix, chan_dh, gate_halo, early = together(mix, chan_dh, gate_halo, early)
+    mix, chan_dh, gate_halo = together(mix, chan_dh, gate_halo)
     filt = swap_blocks(as_chunks(chan_dh))
-    mix_halo = passed_along(mix[:, :HALO, :], "ctx", -1)
-    late = mix_tap_sums(mix, features, projections, edges, groups)
-    late = butterfly_sum(late, "ctx")
-    proj_grads = proj_grads_of(mix, mix_halo, gate_grad, gate_halo, features, feat_halo, per_chan)
-    short_grads = jnp.concatenate([early[spread : spread + KS], late[: 2 * KS]], axis=0)
-    return (
-        output,
-        proj_grads,
-        short_grads.reshape(3, KS, groups),
-        from_chunks(filt),
-        early[:spread].reshape(local),
-    )
+    rows = mix_tap_sums(mix, features, projections, edges, groups)
+    rows = group_sum(rows, "ctx", (1, 2))
+    proj_grads = proj_grads_of(mix, gate_grad, gate_halo, features, feat_halo, per_chan)
+    rows = group_sum(rows, "ctx", (4, 8))
+    filt, proj_grads = together(filt, proj_grads)
+    short_grads = jnp.stack([early[spread : spread + KS], rows[:KS], rows[KS : 2 * KS]])
+    return (output, proj_grads, short_grads, from_chunks(filt), early[:spread].reshape(local))
 
 
 def on_device(projections, grouped_short_filters, long_filter, norm_gain, out_grad):
@@ -1012,7 +1010,7 @@
     width = local // spread
     length = tokens * spread
     whole_tiles = width % LANES == 0 and tokens == LANES and length % BLOCK == 0
-    pairs = spread & (spread - 1) == 0 and lax.axis_size("ch") == 2
+    pairs = spread == 16 and lax.axis_size("ch") == 2
     fits = whole_tiles and pairs and length <= 8 * BLOCK and width == local // GROUP
     path = kernel_path if fits else narrow_path
     return path(projections, grouped_short_filters, long_filter, norm_gain, out_grad)

time: 236 us -> 251 us (1.064)
  waiting for transfers between devices: 82.3 us -> 99.5 us
  starting transfers between devices: 68 us -> 65.4 us
    ppermute x9 -> x12, waiting for transfers between devices: 20.4 us -> 36.6 us  [exchange(): return lax.ppermute(values, axis, [(i, i ^ distance) for i in range(size)])]
    ppermute x9 -> x12, starting transfers between devices: 20.2 us -> 15.6 us  [exchange(): return lax.ppermute(values, axis, [(i, i ^ distance) for i in range(size)])]
    all_to_all x6, starting transfers between devices: 41.5 us -> 44.8 us  [swap_blocks(): lax.all_to_all(chunks, 'ctx', split_axis=0, concat_axis=0, tiled=True)]
    ppermute x4 -> x3, starting transfers between devices: 6.26 us -> 4.98 us  [passed_along(): return lax.ppermute(block, axis, route)]
  transfers between devices with their start and end apart: 19 -> 21, of which waited for: 13 -> 12; matrix products, arithmetic and copies ran while one was open for 1% -> 1% of each run, Pallas kernels for 21% -> 20%
where the time goes in v2:
time: 251 us; the launch traced here: 250 us
  waiting for transfers between devices  99.5 us (40%)
  Pallas kernels  79.1 us (32%)
  starting transfers between devices  65.4 us (26%)
  local copies, waits for them, and re-layouts  4.06 us (2%)
    pallas_call x14, Pallas kernels, whole(): pl.pallas_call(body, in_specs=[ANY if i in streams else VMEM for i in ran...  79.1 us
    all_to_all x6, waiting for transfers between devices, swap_blocks(): lax.all_to_all(chunks, 'ctx', split_axis=0, concat_axis=0, tiled=True)  62.9 us
    all_to_all x6, starting transfers between devices, swap_blocks(): lax.all_to_all(chunks, 'ctx', split_axis=0, concat_axis=0, tiled=True)  44.8 us
    ppermute x12, waiting for transfers between devices, exchange(): return lax.ppermute(values, axis, [(i, i ^ distance) for i in range(size)])  36.6 us
    ppermute x12, starting transfers between devices, exchange(): return lax.ppermute(values, axis, [(i, i ^ distance) for i in range(size)])  15.6 us
  transfers between devices with their start and end apart: 21, of which 12 were waited for; matrix products, arithmetic and copies ran while one was open for 1% of the time, Pallas kernels for 20%

profile of v2, /device:TPU:0, one launch (start us, length us, event | category | flops | bytes accessed | tf_op | source)
XLA Modules:
  0.0 249.9 jit_solution(1105098026890129433)
XLA Ops:
  0.6 0.9 slice.21
  1.6 2.4 collective-permute-start
  4.0 2.5 %shard_map.128 = bf16[16,128,256]{2,1,0:T(8,128)(2,1)} custom-call(f32[128,4096]{1,0:T(8,128)} %source.1), custom_call_target="tpu_custom_call" | custom-call | bytes 3145728 | tf_op jit(solution)/shard_map/pallas_call | solution.py:207
  6.6 9.4 %all-to-all-start = ((bf16[16,128,256]{2,1,0:T(8,128)(2,1)}), bf16[16,128,256]{2,1,0:T(8,128)(2,1)S(1)}, u32[]{:S(2)}, u32[]{:S(2)}) async-start(bf16[16,128,256]{2,1,0:T(8,128)(2,1)} %shard_map.128), calls=%async_computation | async-start | bytes 2097152 | tf_op jit(solution)/shard_map/all_to_all | solution.py:944
  16.0 3.2 %shard_map.129.t_ref = f32[24,4096]{1,0:T(8,128)S(1)} custom-call(f32[24,256]{1,0:T(8,128)S(1)} %pad.4.t_ref), custom_call_target="tpu_custom_call" | custom-call | flops 100663296 | bytes 417792 | tf_op jit(solution)/shard_map/pallas_call | solution.py:207
  19.2 6.1 %shard_map.130 = (bf16[3,128,4096]{2,1,0:T(8,128)(2,1)}, bf16[16,128,256]{2,1,0:T(8,128)(2,1)}) custom-call(bf16[3,128,4096]{2,1,0:T(8,128)(2,1)} %p_hbm.5, bf16[3,8,4096]{2,1,0:T(8,128)(2,1)S(1)} %collective-permute-done.e_ref, f32[24,4096]{1,0:T(8,128)S(1)} %shard_map.129.t_ref), custom_call_target="tpu_custom_call" | custom-call | flops 22020096 | bytes 7929856 | tf_op jit(solution)/shard_map/pallas_call | solution.py:207
  25.4 13.5 %all-to-all-done = bf16[16,128,256]{2,1,0:T(8,128)(2,1)S(1)} async-done(((bf16[16,128,256]{2,1,0:T(8,128)(2,1)}), bf16[16,128,256]{2,1,0:T(8,128)(2,1)S(1)}, u32[]{:S(2)}, u32[]{:S(2)}) %all-to-all-start) | async-done | bytes 1048608 | tf_op jit(solution)/shard_map/all_to_all | solution.py:944
  38.9 6.8 %all-to-all-start.1 = ((bf16[16,128,256]{2,1,0:T(8,128)(2,1)}), bf16[16,128,256]{2,1,0:T(8,128)(2,1)S(1)}, u32[]{:S(2)}, u32[]{:S(2)}) async-start(bf16[16,128,256]{2,1,0:T(8,128)(2,1)} %get-tuple-element.40), calls=%async_computation.1 | async-start | bytes 2097152 | tf_op jit(solution)/shard_map/all_to_all | solution.py:944
  45.7 0.9 slice.22
  46.6 1.3 collective-permute-start.1
  47.9 5.7 %shard_map.131.refs_1_ = f32[8,512,256]{2,1,0:T(8,128)} custom-call(bf16[8,256,256]{2,1,0:T(8,128)(2,1)S(1)} %bitcast.14, bf16[512,256]{1,0:T(8,128)(2,1)} %constant.11.clone.hi_hbm.refs_2_, bf16[512,256]{1,0:T(8,128)(2,1)} %constant.12.clone.lo_hbm.refs_3_), custom_call_target="tpu_custom_call" | custom-call | flops 1073741824 | bytes 5767168 | tf_op jit(solution)/shard_map/pallas_call | solution.py:207
  53.7 14.9 %all-to-all-done.1 = bf16[16,128,256]{2,1,0:T(8,128)(2,1)S(1)} async-done(((bf16[16,128,256]{2,1,0:T(8,128)(2,1)}), bf16[16,128,256]{2,1,0:T(8,128)(2,1)S(1)}, u32[]{:S(2)}, u32[]{:S(2)}) %all-to-all-start.1) | async-done | bytes 1048608 | tf_op jit(solution)/shard_map/all_to_all | solution.py:944
  68.6 10.2 %shard_map.132 = bf16[16,128,256]{2,1,0:T(8,128)(2,1)} custom-call(bf16[8,256,256]{2,1,0:T(8,128)(2,1)S(1)} %bitcast.15, f32[8,512,256]{2,1,0:T(8,128)} %shard_map.131.refs_1_, bf16[512,256]{1,0:T(8,128)(2,1)} %constant.11.clone.hi_hbm.refs_2_, bf16[512,256]{1,0:T(8,128)(2,1)} %constant.12.clone.lo_hbm.refs_3_, ...), custom_call_target="tpu_custom_call" | custom-call | flops 2684354560 | bytes 7340032 | tf_op jit(solution)/shard_map/pallas_call | solution.py:207
  78.8 8.0 %all-to-all-start.2 = ((bf16[16,128,256]{2,1,0:T(8,128)(2,1)}), bf16[16,128,256]{2,1,0:T(8,128)(2,1)S(1)}, u32[]{:S(2)}, u32[]{:S(2)}) async-start(bf16[16,128,256]{2,1,0:T(8,128)(2,1)} %shard_map.132), calls=%async_computation.2 | async-start | bytes 2097152 | tf_op jit(solution)/shard_map/all_to_all | solution.py:944
  86.8 5.7 %shard_map.133.refs_1_ = f32[8,512,256]{2,1,0:T(8,128)} custom-call(bf16[8,256,256]{2,1,0:T(8,128)(2,1)S(1)} %bitcast.16, bf16[512,256]{1,0:T(8,128)(2,1)} %constant.11.clone.hi_hbm.refs_2_, bf16[512,256]{1,0:T(8,128)(2,1)} %constant.12.clone.lo_hbm.refs_3_), custom_call_target="tpu_custom_call" | custom-call | flops 1073741824 | bytes 5767168 | tf_op jit(solution)/shard_map/pallas_call | solution.py:207
  92.5 17.2 %all-to-all-done.2.c_hbm = bf16[16,128,256]{2,1,0:T(8,128)(2,1)S(1)} async-done(((bf16[16,128,256]{2,1,0:T(8,128)(2,1)}), bf16[16,128,256]{2,1,0:T(8,128)(2,1)S(1)}, u32[]{:S(2)}, u32[]{:S(2)}) %all-to-all-start.2) | async-done | bytes 1048608 | tf_op jit(solution)/shard_map/all_to_all | solution.py:944
  109.7 3.1 %shard_map.134 = (f32[8,128]{1,0:T(8,128)S(1)}, bf16[16,128,256]{2,1,0:T(8,128)(2,1)S(1)}, bf16[16,128,256]{2,1,0:T(8,128)(2,1)S(1)}, bf16[16,128,256]{2,1,0:T(8,128)(2,1)S(1)}) custom-call(bf16[3,128,4096]{2,1,0:T(8,128)(2,1)} %get-tuple-element.37.q_hbm.f_hbm, bf16[16,128,256]{2,1,0:T(8,128)(2,1)S(1)} %all-to-all-done.2.c_hbm, f32[1,4096]{1,0:T(1,128)S(1)} %bitcast.18, ...), custom_call_target="tpu_custom_call" | custom-call | flops 3145728 | bytes 8409088 | tf_op jit(solution)/shard_map/pallas_call | solution.py:207
  112.8 1.6 collective-permute-start.2
  114.3 2.1 collective-permute-done.2.r_ref
  116.5 1.9 shard_map.135
  118.3 6.8 %all-to-all-start.3 = ((bf16[16,128,256]{2,1,0:T(8,128)(2,1)}), bf16[16,128,256]{2,1,0:T(8,128)(2,1)S(1)}, u32[]{:S(2)}, u32[]{:S(2)}) async-start(bf16[16,128,256]{2,1,0:T(8,128)(2,1)} %get-tuple-element.49), calls=%async_computation.3 | async-start | bytes 2097152 | tf_op jit(solution)/shard_map/all_to_all | solution.py:944
  125.2 0.7 copy-done.1
  125.8 6.0 %shard_map.136 = (bf16[128,4096]{1,0:T(8,128)(2,1)}, bf16[128,4096]{1,0:T(8,128)(2,1)}, f32[24,256]{1,0:T(8,128)S(1)}) custom-call(bf16[3,128,4096]{2,1,0:T(8,128)(2,1)} %get-tuple-element.37.q_hbm.f_hbm, bf16[16,128,256]{2,1,0:T(8,128)(2,1)S(1)} %all-to-all-done.2.c_hbm, f32[1,4096]{1,0:T(1,128)S(1)} %bitcast.20, bf16[128,4096]{1,0:T(8,128)(2,1)} %o_hbm.3, ...), custom_call_target="tpu_custom_call" | custom-call | flops 14680064 | bytes 10727424 | tf_op jit(solution)/shard_map/pallas_call | solution.py:207
  132.3 1.6 collective-permute-start.4
  134.0 2.4 collective-permute-done.4
  136.4 0.9 collective-permute-done.5
  137.4 2.5 %collective-permute-start.6 = (f32[24,256]{1,0:T(8,128)S(1)}, f32[24,256]{1,0:T(8,128)S(1)}, u32[]{:S(2)}, u32[]{:S(2)}) collective-permute-start(f32[24,256]{1,0:T(8,128)S(1)} %add_add_fusion), channel_id=1, source_target_pairs={{0,8},{2,10},{4,12},{6,14},{8,0},{10,2},{12,4},{14,6},{16,24},{18,... | collective-permute-start | bytes 73736 | tf_op jit(solution)/shard_map/ppermute | solution.py:934
  139.9 3.8 %collective-permute-done.6 = f32[24,256]{1,0:T(8,128)S(1)} collective-permute-done((f32[24,256]{1,0:T(8,128)S(1)}, f32[24,256]{1,0:T(8,128)S(1)}, u32[]{:S(2)}, u32[]{:S(2)}) %collective-permute-start.6) | collective-permute-done | bytes 24608 | tf_op jit(solution)/shard_map/ppermute | solution.py:934
  143.7 4.5 %all-to-all-done.3 = bf16[16,128,256]{2,1,0:T(8,128)(2,1)S(1)} async-done(((bf16[16,128,256]{2,1,0:T(8,128)(2,1)}), bf16[16,128,256]{2,1,0:T(8,128)(2,1)S(1)}, u32[]{:S(2)}, u32[]{:S(2)}) %all-to-all-start.3) | async-done | bytes 1048608 | tf_op jit(solution)/shard_map/all_to_all | solution.py:944
  148.2 10.4 %shard_map.137 = (bf16[16,136,256]{2,1,0:T(8,128)(2,1)}, f32[8,512,256]{2,1,0:T(8,128)}) custom-call(bf16[8,256,256]{2,1,0:T(8,128)(2,1)S(1)} %bitcast.17, f32[8,512,256]{2,1,0:T(8,128)} %shard_map.131.refs_1_, bf16[512,256]{1,0:T(8,128)(2,1)} %constant.11.clone.hi_hbm.refs_2_, bf16[512,256]{1,0:T(8,128)(2,1)} %constant.12.clone.lo_hbm.refs_3_, ...), custom_call_target="tpu_custom_call" | custom-call | flops 2684354560 | bytes 11599872 | tf_op jit(solution)/shard_map/pallas_call | solution.py:207
  158.6 6.6 %all-to-all-start.4 = ((bf16[16,136,256]{2,1,0:T(8,128)(2,1)}), bf16[16,136,256]{2,1,0:T(8,128)(2,1)S(1)}, u32[]{:S(2)}, u32[]{:S(2)}) async-start(bf16[16,136,256]{2,1,0:T(8,128)(2,1)} %get-tuple-element.56), calls=%async_computation.4 | async-start | bytes 2228224 | tf_op jit(solution)/shard_map/all_to_all | solution.py:944
  165.3 0.8 slice.23
  166.1 1.3 collective-permute-start.7
  167.4 8.9 %shard_map.138 = bf16[8,256,256]{2,1,0:T(8,128)(2,1)} custom-call(f32[8,512,256]{2,1,0:T(8,128)} %get-tuple-element.57.refs_0_, f32[8,512,256]{2,1,0:T(8,128)} %shard_map.133.refs_1_, bf16[256,512]{1,0:T(8,128)(2,1)} %constant.13.clone.refs_4_.refs_2_, bf16[256,512]{1,0:T(8,128)(2,1)} %constant.14.clone.refs_5_.refs_3_), custom_call_target="tpu_custom_call" | custom-call | flops 3221225472 | bytes 9961472 | tf_op jit(solution)/shard_map/pallas_call | solution.py:207
  176.4 12.8 %all-to-all-done.4.m_hbm = bf16[16,136,256]{2,1,0:T(8,128)(2,1)S(1)} async-done(((bf16[16,136,256]{2,1,0:T(8,128)(2,1)}), bf16[16,136,256]{2,1,0:T(8,128)(2,1)S(1)}, u32[]{:S(2)}, u32[]{:S(2)}) %all-to-all-start.4) | async-done | bytes 1114144 | tf_op jit(solution)/shard_map/all_to_all | solution.py:944
  189.2 7.1 %all-to-all-start.5 = ((bf16[16,128,256]{2,1,0:T(8,128)(2,1)}), bf16[16,128,256]{2,1,0:T(8,128)(2,1)S(1)}, u32[]{:S(2)}, u32[]{:S(2)}) async-start(bf16[16,128,256]{2,1,0:T(8,128)(2,1)} %bitcast.21), calls=%async_computation.5 | async-start | bytes 2097152 | tf_op jit(solution)/shard_map/all_to_all | solution.py:944
  196.4 2.8 %collective-permute-start.8 = (f32[24,256]{1,0:T(8,128)S(1)}, f32[24,256]{1,0:T(8,128)S(1)}, u32[]{:S(2)}, u32[]{:S(2)}) collective-permute-start(f32[24,256]{1,0:T(8,128)S(1)} %add.38), channel_id=1, source_target_pairs={{0,16},{2,18},{4,20},{6,22},{8,24},{10,26},{12,28},{14,30},{16,0},... | collective-permute-start | bytes 73736 | tf_op jit(solution)/shard_map/ppermute | solution.py:934
  199.2 24.7 %collective-permute-done.8 = f32[24,256]{1,0:T(8,128)S(1)} collective-permute-done((f32[24,256]{1,0:T(8,128)S(1)}, f32[24,256]{1,0:T(8,128)S(1)}, u32[]{:S(2)}, u32[]{:S(2)}) %collective-permute-start.8) | collective-permute-done | bytes 24608 | tf_op jit(solution)/shard_map/ppermute | solution.py:934
  223.9 5.5 %shard_map.140 = f32[16,256]{1,0:T(8,128)S(1)} custom-call(bf16[16,136,256]{2,1,0:T(8,128)(2,1)S(1)} %all-to-all-done.4.m_hbm, bf16[3,128,4096]{2,1,0:T(8,128)(2,1)} %get-tuple-element.37.q_hbm.f_hbm, bf16[3,128,4096]{2,1,0:T(8,128)(2,1)} %p_hbm.5, bf16[3,8,4096]{2,1,0:T(8,128)(2,1)S(1)} %collective-permute-done.e_ref), custom_call_target="tpu_custom_call" | custom-call | flops 14680064 | bytes 7618560 | tf_op jit(solution)/shard_map/pallas_call | solution.py:207
  229.5 1.5 collective-permute-start.10
  231.0 0.7 collective-permute-start.9
  231.7 1.6 collective-permute-done.10
  233.3 0.9 collective-permute-done.11
  234.2 2.0 collective-permute-start.13
  236.3 2.4 collective-permute-start.14
  238.6 0.6 copy.14
  239.2 6.9 %shard_map.139 = bf16[3,128,4096]{2,1,0:T(8,128)(2,1)} custom-call(bf16[16,136,256]{2,1,0:T(8,128)(2,1)S(1)} %all-to-all-done.4.m_hbm, bf16[128,4096]{1,0:T(8,128)(2,1)} %get-tuple-element.61.gg_hbm, bf16[8,4096]{1,0:T(8,128)(2,1)S(1)} %collective-permute-done.7.gh_ref, bf16[3,128,4096]{2,1,0:T(8,128)(2,1)} %get-tuple-element.37.q_hbm.f_hbm, ...), custom_call_target="tpu_custom_call" | custom-call | flops 25165824 | bytes 9109504 | tf_op jit(solution)/shard_map/pallas_call | solution.py:207
  246.8 2.9 %shard_map.141 = f32[128,4096]{1,0:T(8,128)} custom-call(bf16[16,128,256]{2,1,0:T(8,128)(2,1)S(1)} %all-to-all-done.5.source), custom_call_target="tpu_custom_call" | custom-call | bytes 3145728 | tf_op jit(solution)/shard_map/pallas_call | solution.py:207
  (29 shorter events, 1.2 us)
Async XLA Ops:
  0.6 15.4 %copy-start.2 = (f32[3,7,256]{2,1,0:T(8,128)S(1)}, f32[3,7,256]{2,1,0:T(8,128)}, u32[]{:S(2)}) copy-start(f32[3,7,256]{2,1,0:T(8,128)} %param.10) | copy-start | bytes 64516
  1.6 5.0 %collective-permute-start = (bf16[3,8,4096]{2,1,0:T(8,128)(2,1)S(1)}, bf16[3,8,4096]{2,1,0:T(8,128)(2,1)S(1)}, u32[]{:S(2)}, u32[]{:S(2)}) collective-permute-start(bf16[3,8,4096]{2,1,0:T(8,128)(2,1)S(1)} %slice.21), channel_id=1, source_target_pairs={{0,2},{2,4},{4,6},{6,8},{8,10},{10,12},{12,14},{14,16},{16,18},{18... | collective-permute-start | bytes 589832 | tf_op jit(solution)/shard_map/ppermute | solution.py:25
  6.6 32.3 %all-to-all-start = ((bf16[16,128,256]{2,1,0:T(8,128)(2,1)}), bf16[16,128,256]{2,1,0:T(8,128)(2,1)S(1)}, u32[]{:S(2)}, u32[]{:S(2)}) async-start(bf16[16,128,256]{2,1,0:T(8,128)(2,1)} %shard_map.128), calls=%async_computation | async-start | bytes 2097152 | tf_op jit(solution)/shard_map/all_to_all | solution.py:944
  38.9 29.7 %all-to-all-start.1 = ((bf16[16,128,256]{2,1,0:T(8,128)(2,1)}), bf16[16,128,256]{2,1,0:T(8,128)(2,1)S(1)}, u32[]{:S(2)}, u32[]{:S(2)}) async-start(bf16[16,128,256]{2,1,0:T(8,128)(2,1)} %get-tuple-element.40), calls=%async_computation.1 | async-start | bytes 2097152 | tf_op jit(solution)/shard_map/all_to_all | solution.py:944
  46.6 7.0 %collective-permute-start.1 = (bf16[3,8,4096]{2,1,0:T(8,128)(2,1)S(1)}, bf16[3,8,4096]{2,1,0:T(8,128)(2,1)S(1)}, u32[]{:S(2)}, u32[]{:S(2)}) collective-permute-start(bf16[3,8,4096]{2,1,0:T(8,128)(2,1)S(1)} %slice.22), channel_id=1, source_target_pairs={{2,0},{4,2},{6,4},{8,6},{10,8},{12,10},{14,12},{16,14},{18,16},{20... | collective-permute-start | bytes 589832 | tf_op jit(solution)/shard_map/ppermute | solution.py:25
  78.8 30.9 %all-to-all-start.2 = ((bf16[16,128,256]{2,1,0:T(8,128)(2,1)}), bf16[16,128,256]{2,1,0:T(8,128)(2,1)S(1)}, u32[]{:S(2)}, u32[]{:S(2)}) async-start(bf16[16,128,256]{2,1,0:T(8,128)(2,1)} %shard_map.132), calls=%async_computation.2 | async-start | bytes 2097152 | tf_op jit(solution)/shard_map/all_to_all | solution.py:944
  86.8 22.9 %copy-start = (f32[4096]{0:T(1024)S(1)}, f32[4096]{0:T(1024)}, u32[]{:S(2)}) copy-start(f32[4096]{0:T(1024)} %param.12) | copy-start | bytes 49156
  112.8 3.7 %collective-permute-start.2 = (f32[8,128]{1,0:T(8,128)S(1)}, f32[8,128]{1,0:T(8,128)S(1)}, u32[]{:S(2)}, u32[]{:S(2)}) collective-permute-start(f32[8,128]{1,0:T(8,128)S(1)} %get-tuple-element.48.s_ref), channel_id=1, source_target_pairs={{0,1},{1,0},{2,3},{3,2},{4,5},{5,4},{6,7},{7,6},{8,9},{9,8},{10,11... | collective-permute-start | bytes 12296 | tf_op jit(solution)/shard_map/ppermute | solution.py:934
  118.3 29.9 %all-to-all-start.3 = ((bf16[16,128,256]{2,1,0:T(8,128)(2,1)}), bf16[16,128,256]{2,1,0:T(8,128)(2,1)S(1)}, u32[]{:S(2)}, u32[]{:S(2)}) async-start(bf16[16,128,256]{2,1,0:T(8,128)(2,1)} %get-tuple-element.49), calls=%async_computation.3 | async-start | bytes 2097152 | tf_op jit(solution)/shard_map/all_to_all | solution.py:944
  125.2 0.7 copy-start.1
  131.9 2.1 collective-permute-start.3
  132.3 4.1 %collective-permute-start.4 = (f32[24,256]{1,0:T(8,128)S(1)}, f32[24,256]{1,0:T(8,128)S(1)}, u32[]{:S(2)}, u32[]{:S(2)}) collective-permute-start(f32[24,256]{1,0:T(8,128)S(1)} %get-tuple-element.53), channel_id=1, source_target_pairs={{0,4},{2,6},{4,0},{6,2},{8,12},{10,14},{12,8},{14,10},{16,20},{18,... | collective-permute-start | bytes 73736 | tf_op jit(solution)/shard_map/ppermute | solution.py:934
  134.0 3.4 %collective-permute-start.5 = (f32[24,256]{1,0:T(8,128)S(1)}, f32[24,256]{1,0:T(8,128)S(1)}, u32[]{:S(2)}, u32[]{:S(2)}) collective-permute-start(f32[24,256]{1,0:T(8,128)S(1)} %get-tuple-element.53), channel_id=1, source_target_pairs={{0,6},{2,4},{4,2},{6,0},{8,14},{10,12},{12,10},{14,8},{16,22},{18,... | collective-permute-start | bytes 73736 | tf_op jit(solution)/shard_map/ppermute | solution.py:934
  137.4 6.3 %collective-permute-start.6 = (f32[24,256]{1,0:T(8,128)S(1)}, f32[24,256]{1,0:T(8,128)S(1)}, u32[]{:S(2)}, u32[]{:S(2)}) collective-permute-start(f32[24,256]{1,0:T(8,128)S(1)} %add_add_fusion), channel_id=1, source_target_pairs={{0,8},{2,10},{4,12},{6,14},{8,0},{10,2},{12,4},{14,6},{16,24},{18,... | collective-permute-start | bytes 73736 | tf_op jit(solution)/shard_map/ppermute | solution.py:934
  158.6 30.6 %all-to-all-start.4 = ((bf16[16,136,256]{2,1,0:T(8,128)(2,1)}), bf16[16,136,256]{2,1,0:T(8,128)(2,1)S(1)}, u32[]{:S(2)}, u32[]{:S(2)}) async-start(bf16[16,136,256]{2,1,0:T(8,128)(2,1)} %get-tuple-element.56), calls=%async_computation.4 | async-start | bytes 2228224 | tf_op jit(solution)/shard_map/all_to_all | solution.py:944
  166.1 10.2 %collective-permute-start.7 = (bf16[8,4096]{1,0:T(8,128)(2,1)S(1)}, bf16[8,4096]{1,0:T(8,128)(2,1)S(1)}, u32[]{:S(2)}, u32[]{:S(2)}) collective-permute-start(bf16[8,4096]{1,0:T(8,128)(2,1)S(1)} %slice.23), channel_id=1, source_target_pairs={{2,0},{4,2},{6,4},{8,6},{10,8},{12,10},{14,12},{16,14},{18,16},{20... | collective-permute-start | bytes 196616 | tf_op jit(solution)/shard_map/ppermute | solution.py:25
  189.2 57.6 %all-to-all-start.5 = ((bf16[16,128,256]{2,1,0:T(8,128)(2,1)}), bf16[16,128,256]{2,1,0:T(8,128)(2,1)S(1)}, u32[]{:S(2)}, u32[]{:S(2)}) async-start(bf16[16,128,256]{2,1,0:T(8,128)(2,1)} %bitcast.21), calls=%async_computation.5 | async-start | bytes 2097152 | tf_op jit(solution)/shard_map/all_to_all | solution.py:944
  196.4 27.6 %collective-permute-start.8 = (f32[24,256]{1,0:T(8,128)S(1)}, f32[24,256]{1,0:T(8,128)S(1)}, u32[]{:S(2)}, u32[]{:S(2)}) collective-permute-start(f32[24,256]{1,0:T(8,128)S(1)} %add.38), channel_id=1, source_target_pairs={{0,16},{2,18},{4,20},{6,22},{8,24},{10,26},{12,28},{14,30},{16,0},... | collective-permute-start | bytes 73736 | tf_op jit(solution)/shard_map/ppermute | solution.py:934
  229.5 3.8 %collective-permute-start.10 = (f32[16,256]{1,0:T(8,128)S(1)}, f32[16,256]{1,0:T(8,128)S(1)}, u32[]{:S(2)}, u32[]{:S(2)}) collective-permute-start(f32[16,256]{1,0:T(8,128)S(1)} %shard_map.140), channel_id=1, source_target_pairs={{0,4},{2,6},{4,0},{6,2},{8,12},{10,14},{12,8},{14,10},{16,20},{18,... | collective-permute-start | bytes 49160 | tf_op jit(solution)/shard_map/ppermute | solution.py:934
  231.0 3.2 %collective-permute-start.11 = (f32[16,256]{1,0:T(8,128)S(1)}, f32[16,256]{1,0:T(8,128)S(1)}, u32[]{:S(2)}, u32[]{:S(2)}) collective-permute-start(f32[16,256]{1,0:T(8,128)S(1)} %shard_map.140), channel_id=1, source_target_pairs={{0,6},{2,4},{4,2},{6,0},{8,14},{10,12},{12,10},{14,8},{16,22},{18,... | collective-permute-start | bytes 49160 | tf_op jit(solution)/shard_map/ppermute | solution.py:934
  231.0 3.2 %collective-permute-start.9 = (f32[16,256]{1,0:T(8,128)S(1)}, f32[16,256]{1,0:T(8,128)S(1)}, u32[]{:S(2)}, u32[]{:S(2)}) collective-permute-start(f32[16,256]{1,0:T(8,128)S(1)} %shard_map.140), channel_id=1, source_target_pairs={{0,2},{2,0},{4,6},{6,4},{8,10},{10,8},{12,14},{14,12},{16,18},{18,... | collective-permute-start | bytes 49160 | tf_op jit(solution)/shard_map/ppermute | solution.py:934
  234.2 11.9 %collective-permute-start.12 = (f32[16,256]{1,0:T(8,128)S(1)}, f32[16,256]{1,0:T(8,128)S(1)}, u32[]{:S(2)}, u32[]{:S(2)}) collective-permute-start(f32[16,256]{1,0:T(8,128)S(1)} %add_add_fusion.2), channel_id=1, source_target_pairs={{0,8},{2,10},{4,12},{6,14},{8,0},{10,2},{12,4},{14,6},{16,24},{18,... | collective-permute-start | bytes 49160 | tf_op jit(solution)/shard_map/ppermute | solution.py:934
  234.2 11.9 %collective-permute-start.13 = (f32[16,256]{1,0:T(8,128)S(1)}, f32[16,256]{1,0:T(8,128)S(1)}, u32[]{:S(2)}, u32[]{:S(2)}) collective-permute-start(f32[16,256]{1,0:T(8,128)S(1)} %add_add_fusion.2), channel_id=1, source_target_pairs={{0,16},{2,18},{4,20},{6,22},{8,24},{10,26},{12,28},{14,30},{16,0},... | collective-permute-start | bytes 49160 | tf_op jit(solution)/shard_map/ppermute | solution.py:934
  236.3 9.9 %collective-permute-start.14 = (f32[16,256]{1,0:T(8,128)S(1)}, f32[16,256]{1,0:T(8,128)S(1)}, u32[]{:S(2)}, u32[]{:S(2)}) collective-permute-start(f32[16,256]{1,0:T(8,128)S(1)} %add_add_fusion.2), channel_id=1, source_target_pairs={{0,24},{2,26},{4,28},{6,30},{8,16},{10,18},{12,20},{14,22},{16,8},... | collective-permute-start | bytes 49160 | tf_op jit(solution)/shard_map/ppermute | solution.py:934
